TPU v7x, 32 devices: a whole 2x2x4 slice. The times are simulated.
32 devices in a mesh: blk: 4 (over y, x), head: 4 (over z), grp: 2 (over core).
Axes of the slice: x: 2, y: 2, z: 4, core: 2. Of those that a mesh axis runs over, the one named last changes fastest.
Arguments:
- t_query: bfloat16 [4096, 4096], P('blk', ('head', 'grp')), may hold values from -80 to 80
- t_key: bfloat16 [4096, 4096], P('blk', ('head', 'grp')), may hold values from -80 to 80
- t_value: bfloat16 [4096, 4096], P('blk', ('head', 'grp')), may hold values from -6 to 6
- t_out: bfloat16 [4096, 4096], P(('head', 'grp')), may hold values from -0.09375 to 0.09375
- s_query: bfloat16 [4096, 2048], P('blk', ('head', 'grp')), may hold values from -80 to 80
- s_key: bfloat16 [4096, 2048], P('blk', ('head', 'grp')), may hold values from -80 to 80
- s_value: bfloat16 [4096, 2048], P('blk', ('head', 'grp')), may hold values from -6 to 6
- s_out: bfloat16 [2048, 4096], P(('head', 'grp')), may hold values from -0.125 to 0.125
- segments: int32 [4096], P('blk'), may hold values from 0 to 1, never falling along the last dimension, each value on 1 to 4032 neighbouring positions
- selection: int32 [64, 16], P('blk'), may hold values from 0 to 63, as said below
Outputs:
- mismatch: float32 [4096, 4096], P('blk', ('head', 'grp'))
- s_dq: float32 [4096, 2048], P('blk', ('head', 'grp'))
- s_dk: float32 [4096, 2048], P('blk', ('head', 'grp'))
- s_dv: float32 [4096, 2048], P('blk', ('head', 'grp'))
Inputs may be any that keep to these rules, and one draw needn't show every extreme that they name: `selection`: entry 0 of row b is b itself; for b >= 32, entry 1 of row b is b - 32; every entry of row b lies between 0 and b; entries of a row may repeat. `segments`: document numbers never fall along the sequence.
All inputs are finite; a program needn't handle non-finite values.
Results may differ from a plain program's by a relative error of at most 0.015.
Values may be sent and summed in bfloat16 or wider, within the bound.
A program may use at most 128 MiB of HBM per device.

v0:
```python
import functools

import jax
import jax.numpy as jnp
from jax import lax
from jax.experimental import pallas as pl
from jax.experimental.pallas import tpu as pltpu
from jax.sharding import PartitionSpec as P

HD = 128
BS = 64
SCALE = HD ** (-0.5)
LOG2E = 1.4426950408889634
MASKED = -1e30
VMEM_LIMIT = 56 * 1024 * 1024

NT = (((1,), (1,)), ((), ()))
TN = (((0,), (0,)), ((), ()))


def dot(a, b, dims=(((1,), (0,)), ((), ()))):
    return lax.dot_general(a, b, dims, preferred_element_type=jnp.float32)


def visible(key_pos, query_pos, first_count):
    low = jnp.where(query_pos < first_count, 0, first_count)
    return (key_pos <= query_pos) & (key_pos >= low)


def teacher_kernel(tile, info_ref, q_ref, k_ref, v_ref, o_ref):
    offset, first_count = info_ref[0], info_ref[1]
    q_tile = q_ref.shape[0]
    q_start = offset + pl.program_id(1) * q_tile
    q_end = q_start + q_tile
    queries = q_ref[...]

    def step(index, carried, masked):
        largest, total, acc = carried
        rows = pl.ds(pl.multiple_of(index * tile, tile), tile)
        scores = dot(k_ref[rows, :], queries, NT)
        if masked:
            key_pos = index * tile + lax.broadcasted_iota(jnp.int32, scores.shape, 0)
            query_pos = q_start + lax.broadcasted_iota(jnp.int32, (1, q_tile), 1)
            scores = jnp.where(visible(key_pos, query_pos, first_count), scores, MASKED)
        new = jnp.maximum(largest, jnp.max(scores, axis=0, keepdims=True))
        weights = jnp.exp2((scores - new) * (SCALE * LOG2E))
        if masked:
            weights = jnp.where(scores > 0.5 * MASKED, weights, 0.0)
        factor = jnp.exp2((largest - new) * (SCALE * LOG2E))
        total = total * factor + jnp.sum(weights, axis=0, keepdims=True)
        acc = acc * factor + dot(v_ref[rows, :], weights.astype(jnp.bfloat16), TN)
        return new, total, acc

    first = jnp.where(q_start >= first_count, first_count // tile, 0)
    last = (q_end + tile - 1) // tile
    straddles = first_count < q_end

    def general(index, carried):
        low, high = index * tile, (index + 1) * tile
        need = (high > q_start) | ((low < first_count) & straddles)
        return lax.cond(
            need,
            lambda c: step(index, c, True),
            lambda c: step(index, c, False),
            carried,
        )

    carried = (
        jnp.full((1, q_tile), MASKED, jnp.float32),
        jnp.zeros((1, q_tile), jnp.float32),
        jnp.zeros((HD, q_tile), jnp.float32),
    )
    _, total, acc = lax.fori_loop(first, last, general, carried)
    o_ref[...] = (acc / total).T.astype(jnp.bfloat16)


def teacher(queries, keys, values, heads, columns, offset, first_count):
    rows, tokens = queries.shape[0], keys.shape[0]
    width = heads * HD
    step, (q_at, k_at, v_at) = columns
    tile = 512
    info = jnp.stack([offset, first_count]).astype(jnp.int32)
    return pl.pallas_call(
        functools.partial(teacher_kernel, tile),
        grid_spec=pltpu.PrefetchScalarGridSpec(
            num_scalar_prefetch=1,
            grid=(heads, rows // tile),
            in_specs=[
                pl.BlockSpec((tile, HD), lambda h, i, s: (i, step * h + q_at)),
                pl.BlockSpec((tokens, HD), lambda h, i, s: (0, step * h + k_at)),
                pl.BlockSpec((tokens, HD), lambda h, i, s: (0, step * h + v_at)),
            ],
            out_specs=pl.BlockSpec((tile, HD), lambda h, i, s: (i, h)),
        ),
        out_shape=jax.ShapeDtypeStruct((rows, width), jnp.bfloat16),
        compiler_params=pltpu.CompilerParams(vmem_limit_bytes=VMEM_LIMIT),
        cost_estimate=pl.CostEstimate(
            flops=2 * rows * tokens * width, bytes_accessed=8 * tokens * width, transcendentals=0
        ),
    )(info, queries, keys, values)


def spread(ref, scratch, heads):
    for h in range(heads):
        cols = slice(h * HD, (h + 1) * HD)
        scratch[h * BS : (h + 1) * BS, cols] = ref[:, cols].astype(scratch.dtype)


def student_weights(sel_ref, place_ref, info_ref, q_wide, k_all, v_all, k_sel, v_sel, pos, heads):
    block = pl.program_id(0)
    count = sel_ref.shape[1]
    offset, first_count = info_ref[0], info_ref[1]
    within = lax.broadcasted_iota(jnp.int32, (BS, 1), 0)
    for e in range(count):
        chosen = sel_ref[block, e]
        source = pl.ds(pl.multiple_of(place_ref[block, e] * BS, BS), BS)
        k_sel[e * BS : (e + 1) * BS, :] = k_all[source, :]
        v_sel[e * BS : (e + 1) * BS, :] = v_all[source, :]
        pos[e * BS : (e + 1) * BS, :] = jnp.broadcast_to(chosen * BS + within, (BS, heads * BS))
    lane = lax.broadcasted_iota(jnp.int32, (1, heads * BS), 1)
    query_pos = offset + block * BS + lax.rem(lane, BS)
    scores = dot(k_sel[...], q_wide[...], NT)
    allowed = visible(pos[...], query_pos, first_count)
    scores = jnp.where(allowed, scores, MASKED)
    largest = jnp.max(scores, axis=0, keepdims=True)
    weights = jnp.exp2((scores - largest) * (SCALE * LOG2E))
    weights = jnp.where(allowed, weights, 0.0)
    return weights, jnp.sum(weights, axis=0, keepdims=True)


def forward_kernel(heads, sel_ref, place_ref, info_ref, q_ref, k_all, v_all, o_ref, q_wide, k_sel, v_sel, pos):
    @pl.when(pl.program_id(0) == 0)
    def _():
        q_wide[...] = jnp.zeros_like(q_wide)

    spread(q_ref, q_wide, heads)
    weights, total = student_weights(
        sel_ref, place_ref, info_ref, q_wide, k_all, v_all, k_sel, v_sel, pos, heads
    )
    weights = (weights / total).astype(jnp.bfloat16)
    blended = dot(weights, v_sel[...], TN)
    for h in range(heads):
        cols = slice(h * HD, (h + 1) * HD)
        o_ref[:, cols] = blended[h * BS : (h + 1) * BS, cols].astype(jnp.bfloat16)


def backward_kernel(
    heads, cycle, sel_ref, place_ref, info_ref, q_ref, g_ref, k_all, v_all, dq_ref, *rest
):
    own_ref, far_refs = rest[0], rest[1:cycle]
    dk_sum, dv_sum, q_wide, g_wide, k_sel, v_sel, pos = rest[cycle:]
    block = pl.program_id(0)

    @pl.when(block == 0)
    def _():
        q_wide[...] = jnp.zeros_like(q_wide)
        g_wide[...] = jnp.zeros_like(g_wide)
        dk_sum[...] = jnp.zeros_like(dk_sum)
        dv_sum[...] = jnp.zeros_like(dv_sum)

    spread(q_ref, q_wide, heads)
    spread(g_ref, g_wide, heads)
    weights, total = student_weights(
        sel_ref, place_ref, info_ref, q_wide, k_all, v_all, k_sel, v_sel, pos, heads
    )
    weights = weights / total
    weight_grad = dot(v_sel[...], g_wide[...], NT)
    row_dots = jnp.sum(weights * weight_grad, axis=0, keepdims=True)
    score_grad = (weights * (weight_grad - row_dots) * SCALE).astype(jnp.bfloat16)
    query_grad = dot(score_grad, k_sel[...], TN)
    for h in range(heads):
        cols = slice(h * HD, (h + 1) * HD)
        dq_ref[:, cols] = query_grad[h * BS : (h + 1) * BS, cols]
    key_grad = dot(score_grad, q_wide[...])
    value_grad = dot(weights.astype(jnp.bfloat16), g_wide[...])
    for e in range(sel_ref.shape[1]):
        target = pl.ds(pl.multiple_of(place_ref[block, e] * BS, BS), BS)
        dk_sum[target, :] += key_grad[e * BS : (e + 1) * BS, :]
        dv_sum[target, :] += value_grad[e * BS : (e + 1) * BS, :]

    @pl.when(block == pl.num_programs(0) - 1)
    def _():
        rows = own_ref.shape[1]
        own_ref[0] = dk_sum[:rows, :]
        own_ref[1] = dv_sum[:rows, :]
        for d in range(1, cycle):
            far_refs[d - 1][0] = dk_sum[d * rows : (d + 1) * rows, :].astype(jnp.bfloat16)
            far_refs[d - 1][1] = dv_sum[d * rows : (d + 1) * rows, :].astype(jnp.bfloat16)


def student_scratch(heads, keys, wides):
    width = heads * HD
    return [pltpu.VMEM((heads * BS, width), jnp.bfloat16)] * wides + [
        pltpu.VMEM((keys, width), jnp.bfloat16),
        pltpu.VMEM((keys, width), jnp.bfloat16),
        pltpu.VMEM((keys, heads * BS), jnp.int32),
    ]


def student_forward(tables, queries, keys, values):
    rows, width = queries.shape
    tokens = keys.shape[0]
    heads = width // HD
    row_block = pl.BlockSpec((BS, width), lambda b, *_: (b, 0))
    whole = pl.BlockSpec((tokens, width), lambda b, *_: (0, 0))
    return pl.pallas_call(
        functools.partial(forward_kernel, heads),
        grid_spec=pltpu.PrefetchScalarGridSpec(
            num_scalar_prefetch=3,
            grid=(rows // BS,),
            in_specs=[row_block, whole, whole],
            out_specs=row_block,
            scratch_shapes=student_scratch(heads, tables[0].shape[1] * BS, 1),
        ),
        out_shape=jax.ShapeDtypeStruct((rows, width), jnp.bfloat16),
        compiler_params=pltpu.CompilerParams(vmem_limit_bytes=VMEM_LIMIT),
        cost_estimate=pl.CostEstimate(
            flops=16 * rows * tokens * width, bytes_accessed=4 * tokens * width, transcendentals=0
        ),
    )(*tables, queries, keys, values)


def student_backward(tables, queries, grads, keys, values):
    rows, width = queries.shape
    tokens = keys.shape[0]
    cycle = tokens // rows
    heads = width // HD
    row_block = pl.BlockSpec((BS, width), lambda b, *_: (b, 0))
    whole = pl.BlockSpec((tokens, width), lambda b, *_: (0, 0))
    pair = pl.BlockSpec((2, rows, width), lambda b, *_: (0, 0, 0))
    return pl.pallas_call(
        functools.partial(backward_kernel, heads, cycle),
        grid_spec=pltpu.PrefetchScalarGridSpec(
            num_scalar_prefetch=3,
            grid=(rows // BS,),
            in_specs=[row_block, row_block, whole, whole],
            out_specs=[row_block] + [pair] * cycle,
            scratch_shapes=[pltpu.VMEM((tokens, width), jnp.float32)] * 2
            + student_scratch(heads, tables[0].shape[1] * BS, 2),
        ),
        out_shape=[
            jax.ShapeDtypeStruct((rows, width), jnp.float32),
            jax.ShapeDtypeStruct((2, rows, width), jnp.float32),
        ]
        + [jax.ShapeDtypeStruct((2, rows, width), jnp.bfloat16)] * (cycle - 1),
        compiler_params=pltpu.CompilerParams(vmem_limit_bytes=VMEM_LIMIT),
        cost_estimate=pl.CostEstimate(
            flops=32 * rows * tokens * width, bytes_accessed=8 * tokens * width, transcendentals=0
        ),
    )(*tables, queries, grads, keys, values)


def project_kernel(s_attn, t_attn, s_out, t_out, o_ref):
    o_ref[0] = (dot(s_attn[...], s_out[...]) - dot(t_attn[...], t_out[...])).astype(jnp.bfloat16)


def project(s_attn, t_attn, s_out, t_out, groups, s_block=0):
    rows = s_attn.shape[0]
    model = s_out.shape[1]
    tile = model // groups
    return pl.pallas_call(
        project_kernel,
        grid=(groups,),
        in_specs=[
            pl.BlockSpec(s_attn.shape, lambda j: (0, 0)),
            pl.BlockSpec(t_attn.shape, lambda j: (0, 0)),
            pl.BlockSpec((s_attn.shape[1], tile), lambda j: (s_block, j)),
            pl.BlockSpec((t_attn.shape[1], tile), lambda j: (0, j)),
        ],
        out_specs=pl.BlockSpec((1, rows, tile), lambda j: (j, 0, 0)),
        out_shape=jax.ShapeDtypeStruct((groups, rows, tile), jnp.bfloat16),
        compiler_params=pltpu.CompilerParams(vmem_limit_bytes=VMEM_LIMIT),
    )(s_attn, t_attn, s_out, t_out)


def from_earlier(rows, distance):
    route = [(i - distance, i) for i in range(distance, lax.axis_size("blk"))]
    return lax.ppermute(rows, "blk", route)


def on_device(t_query, t_key, t_value, t_out, s_query, s_key, s_value, s_out, segments, selection):
    row_count = t_query.shape[0]
    heads = t_query.shape[1] // HD
    cycle = lax.axis_size("blk")
    split = ("head", "grp")
    groups = lax.axis_size("head") * lax.axis_size("grp")
    my_index = lax.axis_index("blk")
    first_row = my_index * row_count
    shard_blocks = row_count // BS

    count = jnp.sum((segments == 0).astype(jnp.int32)).reshape(1)
    first_count = count
    for distance in range(1, cycle):
        route = [(i, (i + distance) % cycle) for i in range(cycle)]
        first_count = first_count + lax.ppermute(count, "blk", route)
    first_count = first_count[0]
    info = jnp.stack([first_row, first_count]).astype(jnp.int32)

    model_cols = s_out.shape[1] // cycle

    def own_cols(weights):
        return lax.dynamic_slice_in_dim(weights, my_index * model_cols, model_cols, 1)

    s_cols, t_cols = own_cols(s_out), own_cols(t_out)
    s_cols_all = lax.all_gather(s_cols, split, axis=0, tiled=True)
    weights = jnp.concatenate([t_cols, s_cols], axis=0)
    mix = lax.psum(dot(weights, s_cols_all, NT).astype(jnp.bfloat16), "blk")

    if heads % cycle == 0:
        packed = jnp.concatenate(
            [rows.reshape(row_count, heads, HD) for rows in (t_query, t_key, t_value)], axis=2
        ).reshape(row_count, 3 * heads * HD)
        packed = lax.all_to_all(packed, "blk", split_axis=1, concat_axis=0, tiled=True)
        packed, s_key, s_value = lax.optimization_barrier((packed, s_key, s_value))
        whole_heads = teacher(
            packed, packed, packed, heads // cycle, (3, (0, 1, 2)), jnp.int32(0), first_count
        )
        t_attn = lax.all_to_all(whole_heads, "blk", split_axis=0, concat_axis=1, tiled=True)
    else:
        t_attn = teacher(
            t_query,
            lax.all_gather(t_key, "blk", axis=0, tiled=True),
            lax.all_gather(t_value, "blk", axis=0, tiled=True),
            heads,
            (1, (0, 0, 0)),
            first_row,
            first_count,
        )

    key_stack = jnp.concatenate([s_key] + [from_earlier(s_key, d) for d in range(1, cycle)])
    value_stack = jnp.concatenate([s_value] + [from_earlier(s_value, d) for d in range(1, cycle)])
    place = (my_index - selection // shard_blocks) * shard_blocks + selection % shard_blocks
    tables = (selection, place, info)
    s_attn = student_forward(tables, s_query, key_stack, value_stack)

    ratio = t_attn.shape[1] // s_attn.shape[1]
    grad_terms = project(s_attn, t_attn, mix, mix, groups, ratio)
    grads = lax.psum_scatter(grad_terms, split, scatter_dimension=0, tiled=False)
    terms = project(s_attn, t_attn, s_out, t_out, groups)
    terms, grads = lax.optimization_barrier((terms, grads))
    mismatch = lax.psum_scatter(terms, split, scatter_dimension=0, tiled=False)

    grad_query, own, *far = student_backward(
        tables, s_query, grads, key_stack, value_stack
    )
    for distance in range(1, cycle):
        route = [(i, i - distance) for i in range(distance, cycle)]
        own = own + lax.ppermute(far[distance - 1], "blk", route).astype(jnp.float32)
    return (mismatch.astype(jnp.float32), grad_query, own[0], own[1])


def solution(mesh):
    split = ("head", "grp")
    tokens, weights = P("blk", split), P(split, None)
    return jax.shard_map(
        on_device,
        mesh=mesh,
        in_specs=(
            tokens, tokens, tokens, weights, tokens, tokens, tokens, weights, P("blk"),
            P("blk", None),
        ),
        out_specs=(tokens,) * 4,
        check_vma=False,
    )
```

profile of v0, /device:TPU:0, one launch (start us, length us, event | category | flops | bytes accessed | tf_op | source)
XLA Modules:
  0.0 349.7 jit_solution(7636915416026758186)
XLA Ops:
  7.3 2.0 constant_dynamic-slice_fusion
  9.5 0.4 copy_bitcast_fusion.1
  9.9 2.2 pad_maximum_fusion
  12.1 5.3 %all-to-all-start = ((bf16[1024,4,384]{2,0,1:T(8,128)(2,1)}), bf16[1024,4,384]{2,0,1:T(8,128)(2,1)}, u32[]{:S(2)}, u32[]{:S(2)}) async-start(bf16[1024,4,384]{2,0,1:T(8,128)(2,1)} %pad_maximum_fusion), calls=%async_computation | async-start | bytes 6291456 | tf_op jit(solution)/shard_map/all_to_all | solution.py:313
  17.5 0.6 convert_reduce_fusion
  18.1 3.4 collective-permute-start.2
  21.5 0.6 collective-permute-start.1
  22.0 0.5 collective-permute-start
  22.6 1.3 constant_dynamic-slice_fusion.1
  23.9 0.6 fusion.5.place_ref
  24.5 31.0 %collective-permute-done = s32[1]{0:T(128)} collective-permute-done((s32[1]{0:T(128)}, s32[1]{0:T(128)}, u32[]{:S(2)}, u32[]{:S(2)}) %collective-permute-start) | collective-permute-done | bytes 36 | tf_op jit(solution)/shard_map/ppermute | solution.py:295
  57.9 0.6 pad_add_fusion.info_ref
  58.5 0.6 pad_add_fusion.1.info_ref
  59.1 3.2 collective-permute-start.5
  62.3 2.1 collective-permute-start.4
  64.4 2.5 collective-permute-start.3
  66.9 2.1 collective-permute-start.7
  69.0 2.1 collective-permute-start.6
  71.1 7.4 %convolution_convert_fusion = bf16[768,2048]{1,0:T(8,128)(2,1)} fusion(bf16[2048,1024]{1,0:T(8,128)(2,1)} %all-gather.2.cloned.1.call-done, bf16[256,1024]{1,0:T(8,128)(2,1)S(1)} %copy-done.2, bf16[512,1024]{1,0:T(8,128)(2,1)S(1)} %constant_dynamic-slice_fusion.1), kind=kOutput, calls=%fused_computation | convolution fusion | flops 3225944064 | bytes 8912896 | tf_op jit(solution)/shard_map/dot_general | solution.py:22
  78.6 29.2 %shard_map.130 = bf16[4096,128]{1,0:T(8,128)(2,1)} custom-call(s32[2]{0:T(128)} %pad_add_fusion.1.info_ref, bf16[4096,384]{1,0:T(8,128)(2,1)} %bitcast.3.q_ref.k_ref.v_ref, bf16[4096,384]{1,0:T(8,128)(2,1)} %bitcast.3.q_ref.k_ref.v_ref, bf16[4096,384]{1,0:T(8,128)(2,1)} %bitcast.3.q_ref.k_ref.v_ref), custom_call_target="tpu_custom_call" | custom-call | flops 4294967296 | bytes 4194304 | tf_op jit(solution)/shard_map/pallas_call | solution.py:83
  107.8 0.8 constant_dynamic-update-slice_fusion.3
  108.6 0.8 constant_dynamic-update-slice_fusion.7
  109.5 3.5 %all-to-all-start.1 = ((bf16[4,1024,128]{2,1,0:T(8,128)(2,1)}), bf16[4,1024,128]{2,1,0:T(8,128)(2,1)S(1)}, u32[]{:S(2)}, u32[]{:S(2)}) async-start(bf16[4,1024,128]{2,1,0:T(8,128)(2,1)} %bitcast.4), calls=%async_computation.1 | async-start | bytes 2097152 | tf_op jit(solution)/shard_map/all_to_all | solution.py:318
  113.0 4.9 %collective-permute-start.8 = (bf16[1024,256]{1,0:T(8,128)(2,1)S(1)}, bf16[1024,256]{1,0:T(8,128)(2,1)S(1)}, u32[]{:S(2)}, u32[]{:S(2)}) collective-permute-start(bf16[1024,256]{1,0:T(8,128)(2,1)S(1)} %copy-done.6), channel_id=1, source_target_pairs={{0,24},{1,25},{2,26},{3,27},{4,28},{5,29},{6,30},{7,31}} | collective-permute-start | bytes 1572872 | tf_op jit(solution)/shard_map/ppermute | solution.py:278
  118.0 1.9 constant_dynamic-update-slice_fusion.2
  119.8 1.9 constant_dynamic-update-slice_fusion.1
  121.7 1.9 constant_dynamic-update-slice_fusion.k_all
  123.6 1.1 constant_dynamic-update-slice_fusion.6
  124.7 7.4 %collective-permute-done.7 = bf16[1024,256]{1,0:T(8,128)(2,1)} collective-permute-done((bf16[1024,256]{1,0:T(8,128)(2,1)S(1)}, bf16[1024,256]{1,0:T(8,128)(2,1)}, u32[]{:S(2)}, u32[]{:S(2)}) %collective-permute-start.7) | collective-permute-done | bytes 524320 | tf_op jit(solution)/shard_map/ppermute | solution.py:278
  132.1 1.1 constant_dynamic-update-slice_fusion.5
  133.1 1.6 collective-permute-done.8
  134.8 1.3 copy-done.8
  136.1 18.7 %shard_map.129.s_attn = bf16[1024,256]{1,0:T(8,128)(2,1)} custom-call(s32[16,16]{1,0:T(8,128)} %sel_ref.3, s32[16,16]{1,0:T(8,128)} %fusion.5.place_ref, s32[2]{0:T(128)} %pad_add_fusion.info_ref, bf16[1024,256]{1,0:T(8,128)(2,1)} %q_ref.3, bf16[4096,256]{1,0:T(8,128)(2,1)} %constant_dynamic-update-slice_fusion.k_all, bf16[4096,256]{1,0:T(8,128)(2,1)} %copy-done.8), custom_call_target="tpu_custom_call" | custom-call | flops 17179869184 | bytes 4194304 | tf_op jit(solution)/shard_map/pallas_call | solution.py:206
  154.9 1.1 copy_bitcast_fusion.t_attn
  156.0 35.0 %all-reduce.2.cloned.1.call-done.s_out.t_out = bf16[768,2048]{1,0:T(8,128)(2,1)} async-done(((bf16[768,2048]{1,0:T(8,128)(2,1)}), bf16[768,2048]{1,0:T(8,128)(2,1)}) %all-reduce.2.cloned.1.call-update) | async-done | bytes 3145744 | tf_op jit(solution)/shard_map/psum | solution.py:307
  190.9 9.1 %shard_map.132 = bf16[8,1024,256]{2,1,0:T(8,128)(2,1)} custom-call(bf16[1024,256]{1,0:T(8,128)(2,1)} %shard_map.129.s_attn, bf16[1024,512]{1,0:T(8,128)(2,1)} %copy_bitcast_fusion.t_attn, bf16[768,2048]{1,0:T(8,128)(2,1)} %all-reduce.2.cloned.1.call-done.s_out.t_out, bf16[768,2048]{1,0:T(8,128)(2,1)} %all-reduce.2.cloned.1.call-done.s_out.t_out), custom_call_target="tpu_custom_call" | custom-call | tf_op jit(solution)/shard_map/pallas_call | solution.py:261
  200.1 12.4 %shard_map.131 = bf16[8,1024,512]{2,1,0:T(8,128)(2,1)} custom-call(bf16[1024,256]{1,0:T(8,128)(2,1)} %shard_map.129.s_attn, bf16[1024,512]{1,0:T(8,128)(2,1)} %copy_bitcast_fusion.t_attn, bf16[256,4096]{1,0:T(8,128)(2,1)} %s_out.1, bf16[512,4096]{1,0:T(8,128)(2,1)} %t_out.1), custom_call_target="tpu_custom_call" | custom-call | tf_op jit(solution)/shard_map/pallas_call | solution.py:261
  212.5 37.6 %reduce-scatter.3.cloned.1.call-done = bf16[1,1024,256]{2,1,0:T(8,128)(2,1)} async-done(((bf16[8,1024,256]{2,1,0:T(8,128)(2,1)}), bf16[1,1024,256]{2,1,0:T(8,128)(2,1)}) %reduce-scatter.3.cloned.1.call-update) | async-done | bytes 524304 | tf_op jit(solution)/shard_map/reduce_scatter | solution.py:338
  250.2 28.4 %shard_map.133 = (f32[1024,256]{1,0:T(8,128)}, f32[2,1024,256]{2,1,0:T(8,128)}, bf16[2,1024,256]{2,1,0:T(8,128)(2,1)}, bf16[2,1024,256]{2,1,0:T(8,128)(2,1)}, bf16[2,1024,256]{2,1,0:T(8,128)(2,1)}) custom-call(s32[16,16]{1,0:T(8,128)} %sel_ref.3, s32[16,16]{1,0:T(8,128)} %fusion.5.place_ref, s32[2]{0:T(128)} %pad_add_fusion.info_ref, ...), custom_call_target="tpu_custom_call" | custom-call | flops 34359738368 | bytes 8388608 | tf_op jit(solution)/shard_map/pallas_call | solution.py:231
  278.6 1.3 collective-permute-start.9
  279.9 1.3 collective-permute-start.10
  281.2 1.3 collective-permute-start.11
  282.5 21.3 %collective-permute-done.9 = bf16[2,1024,256]{2,1,0:T(8,128)(2,1)S(1)} collective-permute-done((bf16[2,1024,256]{2,1,0:T(8,128)(2,1)}, bf16[2,1024,256]{2,1,0:T(8,128)(2,1)S(1)}, u32[]{:S(2)}, u32[]{:S(2)}) %collective-permute-start.9) | collective-permute-done | bytes 1048608 | tf_op jit(solution)/shard_map/ppermute | solution.py:348
  303.7 24.7 %collective-permute-done.10 = bf16[2,1024,256]{2,1,0:T(8,128)(2,1)S(1)} collective-permute-done((bf16[2,1024,256]{2,1,0:T(8,128)(2,1)}, bf16[2,1024,256]{2,1,0:T(8,128)(2,1)S(1)}, u32[]{:S(2)}, u32[]{:S(2)}) %collective-permute-start.10) | collective-permute-done | bytes 1048608 | tf_op jit(solution)/shard_map/ppermute | solution.py:348
  328.4 2.1 convert_add_fusion
  330.5 1.5 slice_bitcast_fusion
  332.0 8.3 %reduce-scatter.5.cloned.1.call-done = bf16[1,1024,512]{2,1,0:T(8,128)(2,1)} async-done(((bf16[8,1024,512]{2,1,0:T(8,128)(2,1)}), bf16[1,1024,512]{2,1,0:T(8,128)(2,1)}) %reduce-scatter.5.cloned.1.call-update) | async-done | bytes 1048592 | tf_op jit(solution)/shard_map/reduce_scatter | solution.py:341
  340.3 2.8 bitcast_convert_fusion
  (41 shorter events, 0.5 us)
Async XLA Ops:
  7.2 2.3 copy-start
  7.2 2.1 copy-start.3
  7.2 2.3 copy-start.4
  7.2 63.9 %all-gather.2.cloned.1.call-start = ((), (), s32[]{:S(2)}) async-start(), calls=%async_computation.4 | async-start | bytes 4718592 | tf_op jit(solution)/shard_map/all_gather | solution.py:305
  12.1 5.4 %copy-start.10 = (s32[1024]{0:T(1024)S(1)}, s32[1024]{0:T(1024)}, u32[]{:S(2)}) copy-start(s32[1024]{0:T(1024)} %param.18) | copy-start | bytes 12292
  12.1 47.0 %all-to-all-start = ((bf16[1024,4,384]{2,0,1:T(8,128)(2,1)}), bf16[1024,4,384]{2,0,1:T(8,128)(2,1)}, u32[]{:S(2)}, u32[]{:S(2)}) async-start(bf16[1024,4,384]{2,0,1:T(8,128)(2,1)} %pad_maximum_fusion), calls=%async_computation | async-start | bytes 6291456 | tf_op jit(solution)/shard_map/all_to_all | solution.py:313
  17.4 6.5 %copy-start.9 = (s32[16,16]{1,0:T(8,128)S(1)}, s32[16,16]{1,0:T(8,128)}, u32[]{:S(2)}) copy-start(s32[16,16]{1,0:T(8,128)} %sel_ref.3) | copy-start | bytes 3076
  17.4 41.7 %copy-start.5 = (bf16[1024,256]{1,0:T(8,128)(2,1)S(1)}, bf16[1024,256]{1,0:T(8,128)(2,1)}, u32[]{:S(2)}) copy-start(bf16[1024,256]{1,0:T(8,128)(2,1)} %param.15) | copy-start | bytes 1572868
  17.4 49.5 %copy-start.6 = (bf16[1024,256]{1,0:T(8,128)(2,1)S(1)}, bf16[1024,256]{1,0:T(8,128)(2,1)}, u32[]{:S(2)}) copy-start(bf16[1024,256]{1,0:T(8,128)(2,1)} %param.16) | copy-start | bytes 1572868
  17.4 53.7 %copy-start.2 = (bf16[256,1024]{1,0:T(8,128)(2,1)S(1)}, bf16[256,1024]{1,0:T(8,128)(2,1)}, u32[]{:S(2)}) copy-start(bf16[256,1024]{1,0:T(8,128)(2,1)} %constant_dynamic-slice_fusion) | copy-start | bytes 1572868
  17.4 173.5 %all-reduce.2.cloned.1.call-start = ((), (), s32[]{:S(2)}) async-start(), calls=%async_computation.5 | async-start | bytes 6291456 | tf_op jit(solution)/shard_map/psum | solution.py:307
  18.1 39.2 %collective-permute-start.2 = (s32[1]{0:T(128)}, s32[1]{0:T(128)}, u32[]{:S(2)}, u32[]{:S(2)}) collective-permute-start(s32[1]{0:T(128)} %bitcast.1), channel_id=1, source_target_pairs={{0,24},{8,0},{16,8},{24,16},{1,25},{9,1},{17,9},{25,17},{2,26},{10... | collective-permute-start | bytes 20 | tf_op jit(solution)/shard_map/ppermute | solution.py:295
  21.5 35.3 %collective-permute-start.1 = (s32[1]{0:T(128)}, s32[1]{0:T(128)}, u32[]{:S(2)}, u32[]{:S(2)}) collective-permute-start(s32[1]{0:T(128)} %bitcast.1), channel_id=1, source_target_pairs={{0,16},{8,24},{16,0},{24,8},{1,17},{9,25},{17,1},{25,9},{2,18},{10... | collective-permute-start | bytes 20 | tf_op jit(solution)/shard_map/ppermute | solution.py:295
  22.0 33.4 %collective-permute-start = (s32[1]{0:T(128)}, s32[1]{0:T(128)}, u32[]{:S(2)}, u32[]{:S(2)}) collective-permute-start(s32[1]{0:T(128)} %bitcast.1), channel_id=1, source_target_pairs={{0,8},{8,16},{16,24},{24,0},{1,9},{9,17},{17,25},{25,1},{2,10},{10... | collective-permute-start | bytes 20 | tf_op jit(solution)/shard_map/ppermute | solution.py:295
  59.1 62.6 %collective-permute-start.5 = (bf16[1024,256]{1,0:T(8,128)(2,1)S(1)}, bf16[1024,256]{1,0:T(8,128)(2,1)}, u32[]{:S(2)}, u32[]{:S(2)}) collective-permute-start(bf16[1024,256]{1,0:T(8,128)(2,1)S(1)} %copy-done.5), channel_id=1, source_target_pairs={{0,24},{1,25},{2,26},{3,27},{4,28},{5,29},{6,30},{7,31}} | collective-permute-start | bytes 1572872 | tf_op jit(solution)/shard_map/ppermute | solution.py:278
  62.3 57.5 %collective-permute-start.4 = (bf16[1024,256]{1,0:T(8,128)(2,1)S(1)}, bf16[1024,256]{1,0:T(8,128)(2,1)}, u32[]{:S(2)}, u32[]{:S(2)}) collective-permute-start(bf16[1024,256]{1,0:T(8,128)(2,1)S(1)} %copy-done.5), channel_id=1, source_target_pairs={{0,16},{8,24},{1,17},{9,25},{2,18},{10,26},{3,19},{11,27},{4,20},{... | collective-permute-start | bytes 1572872 | tf_op jit(solution)/shard_map/ppermute | solution.py:278
  64.4 48.6 %collective-permute-start.3 = (bf16[1024,256]{1,0:T(8,128)(2,1)S(1)}, bf16[1024,256]{1,0:T(8,128)(2,1)}, u32[]{:S(2)}, u32[]{:S(2)}) collective-permute-start(bf16[1024,256]{1,0:T(8,128)(2,1)S(1)} %copy-done.5), channel_id=1, source_target_pairs={{0,8},{8,16},{16,24},{1,9},{9,17},{17,25},{2,10},{10,18},{18,26},{... | collective-permute-start | bytes 1572872 | tf_op jit(solution)/shard_map/ppermute | solution.py:278
  66.9 65.1 %collective-permute-start.7 = (bf16[1024,256]{1,0:T(8,128)(2,1)S(1)}, bf16[1024,256]{1,0:T(8,128)(2,1)}, u32[]{:S(2)}, u32[]{:S(2)}) collective-permute-start(bf16[1024,256]{1,0:T(8,128)(2,1)S(1)} %copy-done.6), channel_id=1, source_target_pairs={{0,16},{8,24},{1,17},{9,25},{2,18},{10,26},{3,19},{11,27},{4,20},{... | collective-permute-start | bytes 1572872 | tf_op jit(solution)/shard_map/ppermute | solution.py:278
  69.0 54.6 %collective-permute-start.6 = (bf16[1024,256]{1,0:T(8,128)(2,1)S(1)}, bf16[1024,256]{1,0:T(8,128)(2,1)}, u32[]{:S(2)}, u32[]{:S(2)}) collective-permute-start(bf16[1024,256]{1,0:T(8,128)(2,1)S(1)} %copy-done.6), channel_id=1, source_target_pairs={{0,8},{8,16},{16,24},{1,9},{9,17},{17,25},{2,10},{10,18},{18,26},{... | collective-permute-start | bytes 1572872 | tf_op jit(solution)/shard_map/ppermute | solution.py:278
  109.5 45.4 %all-to-all-start.1 = ((bf16[4,1024,128]{2,1,0:T(8,128)(2,1)}), bf16[4,1024,128]{2,1,0:T(8,128)(2,1)S(1)}, u32[]{:S(2)}, u32[]{:S(2)}) async-start(bf16[4,1024,128]{2,1,0:T(8,128)(2,1)} %bitcast.4), calls=%async_computation.1 | async-start | bytes 2097152 | tf_op jit(solution)/shard_map/all_to_all | solution.py:318
  113.0 137.2 %reduce-scatter.3.cloned.1.call-start = ((), (), s32[]{:S(2)}) async-start(), calls=%async_computation.6 | async-start | bytes 4718592 | tf_op jit(solution)/shard_map/reduce_scatter | solution.py:338
  113.0 10.5 %copy-start.7 = (bf16[4096,256]{1,0:T(8,128)(2,1)S(1)}, bf16[4096,256]{1,0:T(8,128)(2,1)}, u32[]{:S(2)}) copy-start(bf16[4096,256]{1,0:T(8,128)(2,1)} %constant_dynamic-update-slice_fusion.7) | copy-start | bytes 6291460
  113.0 21.7 %collective-permute-start.8 = (bf16[1024,256]{1,0:T(8,128)(2,1)S(1)}, bf16[1024,256]{1,0:T(8,128)(2,1)S(1)}, u32[]{:S(2)}, u32[]{:S(2)}) collective-permute-start(bf16[1024,256]{1,0:T(8,128)(2,1)S(1)} %copy-done.6), channel_id=1, source_target_pairs={{0,24},{1,25},{2,26},{3,27},{4,28},{5,29},{6,30},{7,31}} | collective-permute-start | bytes 1572872 | tf_op jit(solution)/shard_map/ppermute | solution.py:278
  134.8 1.3 copy-start.8
  200.1 140.2 %reduce-scatter.5.cloned.1.call-start = ((), (), s32[]{:S(2)}) async-start(), calls=%async_computation.7 | async-start | bytes 9437184 | tf_op jit(solution)/shard_map/reduce_scatter | solution.py:341
  278.6 25.1 %collective-permute-start.9 = (bf16[2,1024,256]{2,1,0:T(8,128)(2,1)}, bf16[2,1024,256]{2,1,0:T(8,128)(2,1)S(1)}, u32[]{:S(2)}, u32[]{:S(2)}) collective-permute-start(bf16[2,1024,256]{2,1,0:T(8,128)(2,1)} %get-tuple-element.21), channel_id=1, source_target_pairs={{8,0},{16,8},{24,16},{9,1},{17,9},{25,17},{10,2},{18,10},{26,18},{... | collective-permute-start | bytes 3145736 | tf_op jit(solution)/shard_map/ppermute | solution.py:348
  279.9 48.5 %collective-permute-start.10 = (bf16[2,1024,256]{2,1,0:T(8,128)(2,1)}, bf16[2,1024,256]{2,1,0:T(8,128)(2,1)S(1)}, u32[]{:S(2)}, u32[]{:S(2)}) collective-permute-start(bf16[2,1024,256]{2,1,0:T(8,128)(2,1)} %get-tuple-element.22), channel_id=1, source_target_pairs={{16,0},{24,8},{17,1},{25,9},{18,2},{26,10},{19,3},{27,11},{20,4},{... | collective-permute-start | bytes 3145736 | tf_op jit(solution)/shard_map/ppermute | solution.py:348
  281.2 47.2 %collective-permute-start.11 = (bf16[2,1024,256]{2,1,0:T(8,128)(2,1)}, bf16[2,1024,256]{2,1,0:T(8,128)(2,1)S(1)}, u32[]{:S(2)}, u32[]{:S(2)}) collective-permute-start(bf16[2,1024,256]{2,1,0:T(8,128)(2,1)} %get-tuple-element.23), channel_id=1, source_target_pairs={{24,0},{25,1},{26,2},{27,3},{28,4},{29,5},{30,6},{31,7}} | collective-permute-start | bytes 3145736 | tf_op jit(solution)/shard_map/ppermute | solution.py:348
  330.5 12.6 %copy-start.1 = (bf16[1024,512]{1,0:T(8,128)(2,1)S(1)}, bf16[1024,512]{1,0:T(8,128)(2,1)}, u32[]{:S(2)}) copy-start(bf16[1024,512]{1,0:T(8,128)(2,1)} %param.11) | copy-start | bytes 3145732
Sparse Core Ops, SparseCore 0:
  10.2 49.5 all-gather.1
  78.7 112.2 all-reduce.1
  200.2 49.8 reduce-scatter.2
  252.3 87.9 reduce-scatter.4
where the time goes:
time: 351 us; the launch traced here: 350 us
  waiting for transfers between devices  167 us (48%)
  Pallas kernels  97.9 us (28%)
  starting transfers between devices  34.3 us (10%)
  local copies, waits for them, and re-layouts  17.2 us (5%)
  between operations  16.4 us (5%)
  other arithmetic  9.57 us (3%)
  matrix products  7.42 us (2%)
    ppermute x3, waiting for transfers between devices, on_device(): lax.ppermute(far[distance - 1], 'blk', route).astype(jnp.float32)  45.9 us
    reduce_scatter x1, waiting for transfers between devices, on_device(): lax.psum_scatter(grad_terms, split, scatter_dimension=0, tiled=False)  37.6 us
    psum x1, waiting for transfers between devices, on_device(): mix = lax.psum(dot(weights, s_cols_all, NT).astype(jnp.bfloat16), 'blk')  35 us
    ppermute x3, waiting for transfers between devices, on_device(): first_count = first_count + lax.ppermute(count, 'blk', route)  31 us
    pallas_call x1, Pallas kernels, teacher(): pl.pallas_call(functools.partial(teacher_kernel, tile), grid_spec=pltpu.P...  29.2 us
    pallas_call x1, Pallas kernels, student_backward(): pl.pallas_call(functools.partial(backward_kernel, heads, cycle), grid_spe...  28.4 us
    pallas_call x2, Pallas kernels, project(): pl.pallas_call(project_kernel, grid=(groups,), in_specs=[pl.BlockSpec(s_a...  21.5 us
    pallas_call x1, Pallas kernels, student_forward(): pl.pallas_call(functools.partial(forward_kernel, heads), grid_spec=pltpu....  18.7 us
  transfers between devices with their start and end apart: 18, of which 8 were waited for; matrix products, arithmetic and copies ran while one was open for 8% of the time, Pallas kernels for 25%

commit v1 on v0

--- a/solution.py
+++ b/solution.py
@@ -254,7 +254,7 @@
     o_ref[0] = (dot(s_attn[...], s_out[...]) - dot(t_attn[...], t_out[...])).astype(jnp.bfloat16)
 
 
-def project(s_attn, t_attn, s_out, t_out, groups, s_block=0):
+def project(s_attn, t_attn, s_out, t_out, groups):
     rows = s_attn.shape[0]
     model = s_out.shape[1]
     tile = model // groups
@@ -264,13 +264,39 @@
         in_specs=[
             pl.BlockSpec(s_attn.shape, lambda j: (0, 0)),
             pl.BlockSpec(t_attn.shape, lambda j: (0, 0)),
-            pl.BlockSpec((s_attn.shape[1], tile), lambda j: (s_block, j)),
+            pl.BlockSpec((s_attn.shape[1], tile), lambda j: (0, j)),
             pl.BlockSpec((t_attn.shape[1], tile), lambda j: (0, j)),
         ],
         out_specs=pl.BlockSpec((1, rows, tile), lambda j: (j, 0, 0)),
         out_shape=jax.ShapeDtypeStruct((groups, rows, tile), jnp.bfloat16),
         compiler_params=pltpu.CompilerParams(vmem_limit_bytes=VMEM_LIMIT),
     )(s_attn, t_attn, s_out, t_out)
+
+
+def project_grads_kernel(t_width, s_attn, t_attn, mix, o_ref):
+    pieces, rows, width = mix.shape
+    columns = mix[...].reshape(pieces * rows, width)
+    o_ref[0] = (
+        dot(s_attn[...], columns[:, t_width:], NT) - dot(t_attn[...], columns[:, :t_width], NT)
+    ).astype(jnp.bfloat16)
+
+
+def project_grads(s_attn, t_attn, mix, groups):
+    rows = s_attn.shape[0]
+    pieces, depth, width = mix.shape
+    tile = depth // groups
+    return pl.pallas_call(
+        functools.partial(project_grads_kernel, t_attn.shape[1]),
+        grid=(groups,),
+        in_specs=[
+            pl.BlockSpec(s_attn.shape, lambda j: (0, 0)),
+            pl.BlockSpec(t_attn.shape, lambda j: (0, 0)),
+            pl.BlockSpec((pieces, tile, width), lambda j: (0, j, 0)),
+        ],
+        out_specs=pl.BlockSpec((1, rows, pieces * tile), lambda j: (j, 0, 0)),
+        out_shape=jax.ShapeDtypeStruct((groups, rows, pieces * tile), jnp.bfloat16),
+        compiler_params=pltpu.CompilerParams(vmem_limit_bytes=VMEM_LIMIT),
+    )(s_attn, t_attn, mix)
 
 
 def from_earlier(rows, distance):
@@ -296,15 +322,11 @@
     first_count = first_count[0]
     info = jnp.stack([first_row, first_count]).astype(jnp.int32)
 
-    model_cols = s_out.shape[1] // cycle
-
-    def own_cols(weights):
-        return lax.dynamic_slice_in_dim(weights, my_index * model_cols, model_cols, 1)
-
-    s_cols, t_cols = own_cols(s_out), own_cols(t_out)
-    s_cols_all = lax.all_gather(s_cols, split, axis=0, tiled=True)
-    weights = jnp.concatenate([t_cols, s_cols], axis=0)
-    mix = lax.psum(dot(weights, s_cols_all, NT).astype(jnp.bfloat16), "blk")
+    piece = s_out.shape[0] // cycle
+    s_rows = lax.dynamic_slice_in_dim(s_out, my_index * piece, piece, 0)
+    s_rows = lax.all_gather(s_rows, split, axis=0, tiled=True)
+    mix = jnp.concatenate([dot(s_rows, t_out, NT), dot(s_rows, s_out, NT)], axis=1)
+    mix = lax.all_gather(mix.astype(jnp.bfloat16), "blk")
 
     if heads % cycle == 0:
         packed = jnp.concatenate(
@@ -333,8 +355,7 @@
     tables = (selection, place, info)
     s_attn = student_forward(tables, s_query, key_stack, value_stack)
 
-    ratio = t_attn.shape[1] // s_attn.shape[1]
-    grad_terms = project(s_attn, t_attn, mix, mix, groups, ratio)
+    grad_terms = project_grads(s_attn, t_attn, mix, groups)
     grads = lax.psum_scatter(grad_terms, split, scatter_dimension=0, tiled=False)
     terms = project(s_attn, t_attn, s_out, t_out, groups)
     terms, grads = lax.optimization_barrier((terms, grads))

time: 351 us -> 341 us (0.972)
  waiting for transfers between devices: 167 us -> 163 us
    all_gather x1 -> x2, waiting for transfers between devices: 0.01 us -> 42.4 us  [the longest x1 42.4 us: on_device(): s_rows = lax.all_gather(s_rows, split, axis=0, tiled=True)]
    psum x1 -> x0, waiting for transfers between devices: 35 us -> none  [on_device(): mix = lax.psum(dot(weights, s_cols_all, NT).astype(jnp.bfloat16), 'blk')]
    ppermute x3, waiting for transfers between devices: 31 us -> 3.38 us  [on_device(): first_count = first_count + lax.ppermute(count, 'blk', route)]
    ppermute x6, waiting for transfers between devices: 9.05 us -> 23.6 us  [from_earlier(): return lax.ppermute(rows, 'blk', route)]
    pallas_call x2 -> x1, Pallas kernels: 21.5 us -> 12.4 us  [project(): pl.pallas_call(project_kernel, grid=(groups,), in_specs=[pl.BlockSpec(s_a...]
    pallas_call x0 -> x1, Pallas kernels: none -> 9.09 us  [project_grads(): pl.pallas_call(functools.partial(project_grads_kernel, t_attn.shape[1]),...]
    unnamed x28 -> x30, local copies, waits for them, and re-layouts: 8.92 us -> 7.88 us
    dot_general x1 -> x2, matrix products: 7.42 us -> 8.37 us  [dot(): return lax.dot_general(a, b, dims, preferred_element_type=jnp.float32)]
where the time goes in v1:
time: 341 us; the launch traced here: 340 us
  waiting for transfers between devices  163 us (48%)
  Pallas kernels  94.8 us (28%)
  starting transfers between devices  32.3 us (9%)
  between operations  16.6 us (5%)
  local copies, waits for them, and re-layouts  15 us (4%)
  other arithmetic  9.68 us (3%)
  matrix products  8.37 us (2%)
    ppermute x3, waiting for transfers between devices, on_device(): lax.ppermute(far[distance - 1], 'blk', route).astype(jnp.float32)  45.9 us
    all_gather x1, waiting for transfers between devices, on_device(): s_rows = lax.all_gather(s_rows, split, axis=0, tiled=True)  42.4 us
    reduce_scatter x1, waiting for transfers between devices, on_device(): lax.psum_scatter(grad_terms, split, scatter_dimension=0, tiled=False)  39.6 us
    pallas_call x1, Pallas kernels, student_backward(): pl.pallas_call(functools.partial(backward_kernel, heads, cycle), grid_spe...  28.4 us
    pallas_call x1, Pallas kernels, teacher(): pl.pallas_call(functools.partial(teacher_kernel, tile), grid_spec=pltpu.P...  26.2 us
    ppermute x6, waiting for transfers between devices, from_earlier(): return lax.ppermute(rows, 'blk', route)  23.6 us
    pallas_call x1, Pallas kernels, student_forward(): pl.pallas_call(functools.partial(forward_kernel, heads), grid_spec=pltpu....  18.7 us
    ppermute x6, starting transfers between devices, from_earlier(): return lax.ppermute(rows, 'blk', route)  15.8 us
  transfers between devices with their start and end apart: 18, of which 8 were waited for; matrix products, arithmetic and copies ran while one was open for 8% of the time, Pallas kernels for 25%

profile of v1, /device:TPU:0, one launch (start us, length us, event | category | flops | bytes accessed | tf_op | source)
XLA Modules:
  0.0 340.1 jit_solution(1530725465717968497)
XLA Ops:
  7.3 2.0 constant_dynamic-slice_fusion
  9.5 0.4 copy_bitcast_fusion.1
  9.9 2.2 pad_maximum_fusion
  12.1 5.3 %all-to-all-start = ((bf16[1024,4,384]{2,0,1:T(8,128)(2,1)}), bf16[1024,4,384]{2,0,1:T(8,128)(2,1)}, u32[]{:S(2)}, u32[]{:S(2)}) async-start(bf16[1024,4,384]{2,0,1:T(8,128)(2,1)} %pad_maximum_fusion), calls=%async_computation | async-start | bytes 6291456 | tf_op jit(solution)/shard_map/all_to_all | solution.py:335
  17.4 42.4 %all-gather.3.cloned.1.call-done = bf16[512,4096]{1,0:T(8,128)(2,1)} async-done(((bf16[64,4096]{1,0:T(8,128)(2,1)}), bf16[512,4096]{1,0:T(8,128)(2,1)}) %all-gather.3.cloned.1.call-update) | async-done | bytes 4194320 | tf_op jit(solution)/shard_map/all_gather | solution.py:327
  59.8 3.6 %fusion.1 = bf16[1,512,256]{1,2,0:T(8,128)(2,1)S(1)} fusion(bf16[512,4096]{1,0:T(8,128)(2,1)} %all-gather.3.cloned.1.call-done, bf16[256,4096]{1,0:T(8,128)(2,1)S(1)} %copy-done.3), kind=kOutput, calls=%fused_computation.5 | convolution fusion | flops 1073872896 | bytes 6553600 | tf_op jit(solution)/shard_map/dot_general | solution.py:22
  63.5 4.7 %fusion = bf16[1,512,512]{1,2,0:T(8,128)(2,1)S(1)} fusion(bf16[512,4096]{1,0:T(8,128)(2,1)} %all-gather.3.cloned.1.call-done, bf16[512,4096]{1,0:T(8,128)(2,1)S(1)} %copy-done.2), kind=kOutput, calls=%fused_computation.3 | convolution fusion | flops 2147745792 | bytes 8912896 | tf_op jit(solution)/shard_map/dot_general | solution.py:22
  68.3 1.2 copy.24
  69.5 0.6 convert_reduce_fusion
  70.1 2.4 collective-permute-start.2
  72.5 0.6 collective-permute-start.1
  73.1 0.6 collective-permute-start
  73.6 0.6 fusion.4.place_ref
  74.2 3.4 collective-permute-done
  80.2 0.7 pad_add_fusion.info_ref
  80.9 0.6 pad_add_fusion.1.info_ref
  81.5 2.0 collective-permute-start.5
  83.5 2.9 collective-permute-start.4
  86.4 2.5 collective-permute-start.3
  88.9 1.3 collective-permute-start.7
  90.2 2.2 collective-permute-start.6
  92.4 26.2 %shard_map.130 = bf16[4096,128]{1,0:T(8,128)(2,1)} custom-call(s32[2]{0:T(128)} %pad_add_fusion.1.info_ref, bf16[4096,384]{1,0:T(8,128)(2,1)} %bitcast.3.q_ref.k_ref.v_ref, bf16[4096,384]{1,0:T(8,128)(2,1)} %bitcast.3.q_ref.k_ref.v_ref, bf16[4096,384]{1,0:T(8,128)(2,1)} %bitcast.3.q_ref.k_ref.v_ref), custom_call_target="tpu_custom_call" | custom-call | flops 4294967296 | bytes 4194304 | tf_op jit(solution)/shard_map/pallas_call | solution.py:83
  118.6 0.8 constant_dynamic-update-slice_fusion.3
  119.4 0.8 constant_dynamic-update-slice_fusion.7
  120.2 3.5 %all-to-all-start.1 = ((bf16[4,1024,128]{2,1,0:T(8,128)(2,1)}), bf16[4,1024,128]{2,1,0:T(8,128)(2,1)S(1)}, u32[]{:S(2)}, u32[]{:S(2)}) async-start(bf16[4,1024,128]{2,1,0:T(8,128)(2,1)} %bitcast.4), calls=%async_computation.1 | async-start | bytes 2097152 | tf_op jit(solution)/shard_map/all_to_all | solution.py:340
  123.8 4.9 %collective-permute-start.8 = (bf16[1024,256]{1,0:T(8,128)(2,1)S(1)}, bf16[1024,256]{1,0:T(8,128)(2,1)S(1)}, u32[]{:S(2)}, u32[]{:S(2)}) collective-permute-start(bf16[1024,256]{1,0:T(8,128)(2,1)S(1)} %copy-done.7), channel_id=1, source_target_pairs={{0,24},{1,25},{2,26},{3,27},{4,28},{5,29},{6,30},{7,31}} | collective-permute-start | bytes 1572872 | tf_op jit(solution)/shard_map/ppermute | solution.py:304
  128.8 1.9 constant_dynamic-update-slice_fusion.2
  130.6 1.9 constant_dynamic-update-slice_fusion.1
  132.5 0.8 constant_dynamic-update-slice_fusion.k_all
  133.3 1.1 constant_dynamic-update-slice_fusion.6
  134.4 16.8 %collective-permute-done.7 = bf16[1024,256]{1,0:T(8,128)(2,1)S(1)} collective-permute-done((bf16[1024,256]{1,0:T(8,128)(2,1)S(1)}, bf16[1024,256]{1,0:T(8,128)(2,1)S(1)}, u32[]{:S(2)}, u32[]{:S(2)}) %collective-permute-start.7) | collective-permute-done | bytes 524320 | tf_op jit(solution)/shard_map/ppermute | solution.py:304
  151.2 6.8 %collective-permute-done.8 = bf16[1024,256]{1,0:T(8,128)(2,1)S(1)} collective-permute-done((bf16[1024,256]{1,0:T(8,128)(2,1)S(1)}, bf16[1024,256]{1,0:T(8,128)(2,1)S(1)}, u32[]{:S(2)}, u32[]{:S(2)}) %collective-permute-start.8) | collective-permute-done | bytes 524320 | tf_op jit(solution)/shard_map/ppermute | solution.py:304
  158.1 1.3 copy-done.9
  159.4 18.7 %shard_map.129.s_attn = bf16[1024,256]{1,0:T(8,128)(2,1)} custom-call(s32[16,16]{1,0:T(8,128)} %sel_ref.3, s32[16,16]{1,0:T(8,128)} %fusion.4.place_ref, s32[2]{0:T(128)} %pad_add_fusion.info_ref, bf16[1024,256]{1,0:T(8,128)(2,1)} %q_ref.3, bf16[4096,256]{1,0:T(8,128)(2,1)} %constant_dynamic-update-slice_fusion.k_all, bf16[4096,256]{1,0:T(8,128)(2,1)} %copy-done.9), custom_call_target="tpu_custom_call" | custom-call | flops 17179869184 | bytes 4194304 | tf_op jit(solution)/shard_map/pallas_call | solution.py:206
  178.1 1.1 copy_bitcast_fusion.t_attn
  179.2 9.1 %shard_map.132 = bf16[8,1024,256]{2,1,0:T(8,128)(2,1)} custom-call(bf16[1024,256]{1,0:T(8,128)(2,1)} %shard_map.129.s_attn, bf16[1024,512]{1,0:T(8,128)(2,1)} %copy_bitcast_fusion.t_attn, bf16[4,512,768]{2,1,0:T(8,128)(2,1)} %all-gather.5.cloned.1.call-done.mix), custom_call_target="tpu_custom_call" | custom-call | tf_op jit(solution)/shard_map/pallas_call | solution.py:288
  188.6 12.4 %shard_map.131 = bf16[8,1024,512]{2,1,0:T(8,128)(2,1)} custom-call(bf16[1024,256]{1,0:T(8,128)(2,1)} %shard_map.129.s_attn, bf16[1024,512]{1,0:T(8,128)(2,1)} %copy_bitcast_fusion.t_attn, bf16[256,4096]{1,0:T(8,128)(2,1)} %s_out.1, bf16[512,4096]{1,0:T(8,128)(2,1)} %t_out.1), custom_call_target="tpu_custom_call" | custom-call | tf_op jit(solution)/shard_map/pallas_call | solution.py:261
  201.0 39.6 %reduce-scatter.3.cloned.1.call-done = bf16[1,1024,256]{2,1,0:T(8,128)(2,1)} async-done(((bf16[8,1024,256]{2,1,0:T(8,128)(2,1)}), bf16[1,1024,256]{2,1,0:T(8,128)(2,1)}) %reduce-scatter.3.cloned.1.call-update) | async-done | bytes 524304 | tf_op jit(solution)/shard_map/reduce_scatter | solution.py:359
  240.6 28.4 %shard_map.133 = (f32[1024,256]{1,0:T(8,128)}, f32[2,1024,256]{2,1,0:T(8,128)}, bf16[2,1024,256]{2,1,0:T(8,128)(2,1)}, bf16[2,1024,256]{2,1,0:T(8,128)(2,1)}, bf16[2,1024,256]{2,1,0:T(8,128)(2,1)}) custom-call(s32[16,16]{1,0:T(8,128)} %sel_ref.3, s32[16,16]{1,0:T(8,128)} %fusion.4.place_ref, s32[2]{0:T(128)} %pad_add_fusion.info_ref, ...), custom_call_target="tpu_custom_call" | custom-call | flops 34359738368 | bytes 8388608 | tf_op jit(solution)/shard_map/pallas_call | solution.py:231
  269.0 1.3 collective-permute-start.9
  270.2 1.3 collective-permute-start.10
  271.5 1.3 collective-permute-start.11
  272.8 21.3 %collective-permute-done.9 = bf16[2,1024,256]{2,1,0:T(8,128)(2,1)S(1)} collective-permute-done((bf16[2,1024,256]{2,1,0:T(8,128)(2,1)}, bf16[2,1024,256]{2,1,0:T(8,128)(2,1)S(1)}, u32[]{:S(2)}, u32[]{:S(2)}) %collective-permute-start.9) | collective-permute-done | bytes 1048608 | tf_op jit(solution)/shard_map/ppermute | solution.py:369
  294.1 24.7 %collective-permute-done.10 = bf16[2,1024,256]{2,1,0:T(8,128)(2,1)S(1)} collective-permute-done((bf16[2,1024,256]{2,1,0:T(8,128)(2,1)}, bf16[2,1024,256]{2,1,0:T(8,128)(2,1)S(1)}, u32[]{:S(2)}, u32[]{:S(2)}) %collective-permute-start.10) | collective-permute-done | bytes 1048608 | tf_op jit(solution)/shard_map/ppermute | solution.py:369
  318.8 2.1 convert_add_fusion
  320.9 1.5 slice_bitcast_fusion
  322.4 8.4 %reduce-scatter.5.cloned.1.call-done = bf16[1,1024,512]{2,1,0:T(8,128)(2,1)} async-done(((bf16[8,1024,512]{2,1,0:T(8,128)(2,1)}), bf16[1,1024,512]{2,1,0:T(8,128)(2,1)}) %reduce-scatter.5.cloned.1.call-update) | async-done | bytes 1048592 | tf_op jit(solution)/shard_map/reduce_scatter | solution.py:362
  330.7 2.8 bitcast_convert_fusion
  (45 shorter events, 0.8 us)
Async XLA Ops:
  7.2 2.3 copy-start
  7.2 2.1 copy-start.4
  7.2 2.3 copy-start.5
  7.2 52.6 %all-gather.3.cloned.1.call-start = ((), (), s32[]{:S(2)}) async-start(), calls=%async_computation.4 | async-start | bytes 4718592 | tf_op jit(solution)/shard_map/all_gather | solution.py:327
  12.1 47.8 %copy-start.3 = (bf16[256,4096]{1,0:T(8,128)(2,1)S(1)}, bf16[256,4096]{1,0:T(8,128)(2,1)}, u32[]{:S(2)}) copy-start(bf16[256,4096]{1,0:T(8,128)(2,1)} %s_out.1) | copy-start | bytes 6291460
  12.1 69.4 %all-to-all-start = ((bf16[1024,4,384]{2,0,1:T(8,128)(2,1)}), bf16[1024,4,384]{2,0,1:T(8,128)(2,1)}, u32[]{:S(2)}, u32[]{:S(2)}) async-start(bf16[1024,4,384]{2,0,1:T(8,128)(2,1)} %pad_maximum_fusion), calls=%async_computation | async-start | bytes 6291456 | tf_op jit(solution)/shard_map/all_to_all | solution.py:335
  17.4 161.8 %all-gather.5.cloned.1.call-start = ((), (), s32[]{:S(2)}) async-start(), calls=%async_computation.5 | async-start | bytes 3932160 | tf_op jit(solution)/shard_map/all_gather | solution.py:329
  59.8 3.6 %copy-start.2 = (bf16[512,4096]{1,0:T(8,128)(2,1)S(1)}, bf16[512,4096]{1,0:T(8,128)(2,1)}, u32[]{:S(2)}) copy-start(bf16[512,4096]{1,0:T(8,128)(2,1)} %t_out.1) | copy-start | bytes 12582916
  68.2 1.3 copy-start.11
  68.2 5.4 %copy-start.10 = (s32[16,16]{1,0:T(8,128)S(1)}, s32[16,16]{1,0:T(8,128)}, u32[]{:S(2)}) copy-start(s32[16,16]{1,0:T(8,128)} %sel_ref.3) | copy-start | bytes 3076
  68.2 13.2 %copy-start.6 = (bf16[1024,256]{1,0:T(8,128)(2,1)S(1)}, bf16[1024,256]{1,0:T(8,128)(2,1)}, u32[]{:S(2)}) copy-start(bf16[1024,256]{1,0:T(8,128)(2,1)} %param.15) | copy-start | bytes 1572868
  68.2 20.6 %copy-start.7 = (bf16[1024,256]{1,0:T(8,128)(2,1)S(1)}, bf16[1024,256]{1,0:T(8,128)(2,1)}, u32[]{:S(2)}) copy-start(bf16[1024,256]{1,0:T(8,128)(2,1)} %param.16) | copy-start | bytes 1572868
  70.1 9.5 %collective-permute-start.2 = (s32[1]{0:T(128)}, s32[1]{0:T(128)}, u32[]{:S(2)}, u32[]{:S(2)}) collective-permute-start(s32[1]{0:T(128)} %bitcast.1), channel_id=1, source_target_pairs={{0,24},{8,0},{16,8},{24,16},{1,25},{9,1},{17,9},{25,17},{2,26},{10... | collective-permute-start | bytes 20 | tf_op jit(solution)/shard_map/ppermute | solution.py:321
  72.5 6.4 %collective-permute-start.1 = (s32[1]{0:T(128)}, s32[1]{0:T(128)}, u32[]{:S(2)}, u32[]{:S(2)}) collective-permute-start(s32[1]{0:T(128)} %bitcast.1), channel_id=1, source_target_pairs={{0,16},{8,24},{16,0},{24,8},{1,17},{9,25},{17,1},{25,9},{2,18},{10... | collective-permute-start | bytes 20 | tf_op jit(solution)/shard_map/ppermute | solution.py:321
  73.1 4.6 %collective-permute-start = (s32[1]{0:T(128)}, s32[1]{0:T(128)}, u32[]{:S(2)}, u32[]{:S(2)}) collective-permute-start(s32[1]{0:T(128)} %bitcast.1), channel_id=1, source_target_pairs={{0,8},{8,16},{16,24},{24,0},{1,9},{9,17},{17,25},{25,1},{2,10},{10... | collective-permute-start | bytes 20 | tf_op jit(solution)/shard_map/ppermute | solution.py:321
  81.5 51.0 %collective-permute-start.5 = (bf16[1024,256]{1,0:T(8,128)(2,1)S(1)}, bf16[1024,256]{1,0:T(8,128)(2,1)S(1)}, u32[]{:S(2)}, u32[]{:S(2)}) collective-permute-start(bf16[1024,256]{1,0:T(8,128)(2,1)S(1)} %copy-done.6), channel_id=1, source_target_pairs={{0,24},{1,25},{2,26},{3,27},{4,28},{5,29},{6,30},{7,31}} | collective-permute-start | bytes 1572872 | tf_op jit(solution)/shard_map/ppermute | solution.py:304
  83.5 47.2 %collective-permute-start.4 = (bf16[1024,256]{1,0:T(8,128)(2,1)S(1)}, bf16[1024,256]{1,0:T(8,128)(2,1)}, u32[]{:S(2)}, u32[]{:S(2)}) collective-permute-start(bf16[1024,256]{1,0:T(8,128)(2,1)S(1)} %copy-done.6), channel_id=1, source_target_pairs={{0,16},{8,24},{1,17},{9,25},{2,18},{10,26},{3,19},{11,27},{4,20},{... | collective-permute-start | bytes 1572872 | tf_op jit(solution)/shard_map/ppermute | solution.py:304
  86.4 37.4 %collective-permute-start.3 = (bf16[1024,256]{1,0:T(8,128)(2,1)S(1)}, bf16[1024,256]{1,0:T(8,128)(2,1)}, u32[]{:S(2)}, u32[]{:S(2)}) collective-permute-start(bf16[1024,256]{1,0:T(8,128)(2,1)S(1)} %copy-done.6), channel_id=1, source_target_pairs={{0,8},{8,16},{16,24},{1,9},{9,17},{17,25},{2,10},{10,18},{18,26},{... | collective-permute-start | bytes 1572872 | tf_op jit(solution)/shard_map/ppermute | solution.py:304
  88.9 62.3 %collective-permute-start.7 = (bf16[1024,256]{1,0:T(8,128)(2,1)S(1)}, bf16[1024,256]{1,0:T(8,128)(2,1)S(1)}, u32[]{:S(2)}, u32[]{:S(2)}) collective-permute-start(bf16[1024,256]{1,0:T(8,128)(2,1)S(1)} %copy-done.7), channel_id=1, source_target_pairs={{0,16},{8,24},{1,17},{9,25},{2,18},{10,26},{3,19},{11,27},{4,20},{... | collective-permute-start | bytes 1572872 | tf_op jit(solution)/shard_map/ppermute | solution.py:304
  90.2 43.1 %collective-permute-start.6 = (bf16[1024,256]{1,0:T(8,128)(2,1)S(1)}, bf16[1024,256]{1,0:T(8,128)(2,1)}, u32[]{:S(2)}, u32[]{:S(2)}) collective-permute-start(bf16[1024,256]{1,0:T(8,128)(2,1)S(1)} %copy-done.7), channel_id=1, source_target_pairs={{0,8},{8,16},{16,24},{1,9},{9,17},{17,25},{2,10},{10,18},{18,26},{... | collective-permute-start | bytes 1572872 | tf_op jit(solution)/shard_map/ppermute | solution.py:304
  120.2 57.9 %all-to-all-start.1 = ((bf16[4,1024,128]{2,1,0:T(8,128)(2,1)}), bf16[4,1024,128]{2,1,0:T(8,128)(2,1)S(1)}, u32[]{:S(2)}, u32[]{:S(2)}) async-start(bf16[4,1024,128]{2,1,0:T(8,128)(2,1)} %bitcast.4), calls=%async_computation.1 | async-start | bytes 2097152 | tf_op jit(solution)/shard_map/all_to_all | solution.py:340
  123.8 116.8 %reduce-scatter.3.cloned.1.call-start = ((), (), s32[]{:S(2)}) async-start(), calls=%async_computation.6 | async-start | bytes 4718592 | tf_op jit(solution)/shard_map/reduce_scatter | solution.py:359
  123.8 9.5 %copy-start.8 = (bf16[4096,256]{1,0:T(8,128)(2,1)S(1)}, bf16[4096,256]{1,0:T(8,128)(2,1)}, u32[]{:S(2)}) copy-start(bf16[4096,256]{1,0:T(8,128)(2,1)} %constant_dynamic-update-slice_fusion.7) | copy-start | bytes 6291460
  123.8 34.2 %collective-permute-start.8 = (bf16[1024,256]{1,0:T(8,128)(2,1)S(1)}, bf16[1024,256]{1,0:T(8,128)(2,1)S(1)}, u32[]{:S(2)}, u32[]{:S(2)}) collective-permute-start(bf16[1024,256]{1,0:T(8,128)(2,1)S(1)} %copy-done.7), channel_id=1, source_target_pairs={{0,24},{1,25},{2,26},{3,27},{4,28},{5,29},{6,30},{7,31}} | collective-permute-start | bytes 1572872 | tf_op jit(solution)/shard_map/ppermute | solution.py:304
  158.1 1.3 copy-start.9
  188.3 142.4 %reduce-scatter.5.cloned.1.call-start = ((), (), s32[]{:S(2)}) async-start(), calls=%async_computation.7 | async-start | bytes 9437184 | tf_op jit(solution)/shard_map/reduce_scatter | solution.py:362
  269.0 25.1 %collective-permute-start.9 = (bf16[2,1024,256]{2,1,0:T(8,128)(2,1)}, bf16[2,1024,256]{2,1,0:T(8,128)(2,1)S(1)}, u32[]{:S(2)}, u32[]{:S(2)}) collective-permute-start(bf16[2,1024,256]{2,1,0:T(8,128)(2,1)} %get-tuple-element.21), channel_id=1, source_target_pairs={{8,0},{16,8},{24,16},{9,1},{17,9},{25,17},{10,2},{18,10},{26,18},{... | collective-permute-start | bytes 3145736 | tf_op jit(solution)/shard_map/ppermute | solution.py:369
  270.2 48.5 %collective-permute-start.10 = (bf16[2,1024,256]{2,1,0:T(8,128)(2,1)}, bf16[2,1024,256]{2,1,0:T(8,128)(2,1)S(1)}, u32[]{:S(2)}, u32[]{:S(2)}) collective-permute-start(bf16[2,1024,256]{2,1,0:T(8,128)(2,1)} %get-tuple-element.22), channel_id=1, source_target_pairs={{16,0},{24,8},{17,1},{25,9},{18,2},{26,10},{19,3},{27,11},{20,4},{... | collective-permute-start | bytes 3145736 | tf_op jit(solution)/shard_map/ppermute | solution.py:369
  271.5 47.2 %collective-permute-start.11 = (bf16[2,1024,256]{2,1,0:T(8,128)(2,1)}, bf16[2,1024,256]{2,1,0:T(8,128)(2,1)S(1)}, u32[]{:S(2)}, u32[]{:S(2)}) collective-permute-start(bf16[2,1024,256]{2,1,0:T(8,128)(2,1)} %get-tuple-element.23), channel_id=1, source_target_pairs={{24,0},{25,1},{26,2},{27,3},{28,4},{29,5},{30,6},{31,7}} | collective-permute-start | bytes 3145736 | tf_op jit(solution)/shard_map/ppermute | solution.py:369
  320.9 12.7 %copy-start.1 = (bf16[1024,512]{1,0:T(8,128)(2,1)S(1)}, bf16[1024,512]{1,0:T(8,128)(2,1)}, u32[]{:S(2)}) copy-start(bf16[1024,512]{1,0:T(8,128)(2,1)} %param.11) | copy-start | bytes 3145732
Sparse Core Ops, SparseCore 0:
  10.2 49.5 all-gather.2
  69.6 87.3 all-gather.4
  188.5 52.0 reduce-scatter.2
  242.7 88.0 reduce-scatter.4

commit v2 on v1

--- a/solution.py
+++ b/solution.py
@@ -304,12 +304,517 @@
     return lax.ppermute(rows, "blk", route)
 
 
+MESH = pl.DeviceIdType.MESH
+
+
+def greet(blk, grp, cycle, cores):
+    barrier = pltpu.get_barrier_semaphore()
+    for d in range(cycle):
+        for e in range(cores):
+            if d or e:
+                pl.semaphore_signal(
+                    barrier,
+                    inc=1,
+                    device_id={"blk": lax.rem(blk + d, cycle), "grp": lax.rem(grp + e, cores)},
+                    device_id_type=MESH,
+                )
+    pl.semaphore_wait(barrier, cycle * cores - 1)
+
+
+def send(src, dst, send_sem, recv_sem, blk, grp):
+    return pltpu.make_async_remote_copy(
+        src_ref=src,
+        dst_ref=dst,
+        send_sem=send_sem,
+        recv_sem=recv_sem,
+        device_id={"blk": blk, "grp": grp},
+        device_id_type=MESH,
+    )
+
+
+def arrive_kernel(
+    cycle, cores, tq, tk, tv, sq, sk, sv, ints,
+    oq, ok, ov, pq, pk, pv, oints,
+    t_stage, s_stage, local, s_send, s_recv, x_send, x_recv, t_send, t_recv, i_send, i_recv,
+):
+    blk, grp = lax.axis_index("blk"), lax.axis_index("grp")
+    rows = tq.shape[0]
+    half = rows // cores
+    share = cycle // cores
+    owner = blk // share
+    greet(blk, grp, cycle, cores)
+
+    def student_copy(t, j, e):
+        src = (sq, sk, sv)[t].at[pl.ds(e * half, half), pl.ds(j * HD, HD)]
+        dst = (pq.at[blk], pk.at[e, blk], pv.at[e, blk])[t]
+        return src, dst
+
+    def student_send(t, j, e):
+        return send(
+            *student_copy(t, j, e), s_send.at[t, j, e], s_recv.at[t, blk], grp * share + j, e
+        )
+
+    pieces = [(t, j, e) for t in (1, 2, 0) for j in range(share) for e in range(cores)]
+    for t, j, e in pieces:
+        mine = (grp * share + j == blk) & (grp == e)
+
+        @pl.when(jnp.logical_not(mine))
+        def _():
+            student_send(t, j, e).start()
+
+    int_copies = [
+        send(ints, oints.at[blk], i_send.at[d - 1], i_recv.at[d - 1], lax.rem(blk + d, cycle), grp)
+        for d in range(1, cycle)
+    ]
+    for copy in int_copies:
+        copy.start()
+    oints[blk] = ints[...]
+
+    t_copies = []
+    for t, (src, dst) in enumerate(((tk, ok), (tv, ov), (tq, oq))):
+        for d in range(1, cycle):
+            dest = lax.rem(blk + d, cycle)
+            columns = pl.ds(pl.multiple_of(dest * HD, HD), HD)
+            t_copies.append(
+                send(
+                    src.at[:, columns], dst.at[blk], t_send.at[t, d - 1], t_recv.at[t, d - 1], dest, grp
+                )
+            )
+    for copy in t_copies:
+        copy.start()
+
+    columns = pl.ds(pl.multiple_of(blk * HD, HD), HD)
+    for t, (src, dst) in enumerate(((tk, ok), (tv, ov), (tq, oq))):
+        pltpu.make_async_copy(src.at[:, columns], t_stage.at[t], local.at[t]).start()
+    for t, (src, dst) in enumerate(((tk, ok), (tv, ov), (tq, oq))):
+        pltpu.make_async_copy(src.at[:, columns], t_stage.at[t], local.at[t]).wait()
+        pltpu.make_async_copy(t_stage.at[t], dst.at[blk], local.at[t]).start()
+    for t, (src, dst) in enumerate(((tk, ok), (tv, ov), (tq, oq))):
+        pltpu.make_async_copy(t_stage.at[t], dst.at[blk], local.at[t]).wait()
+
+    for t, j, e in pieces:
+        mine = (grp * share + j == blk) & (grp == e)
+
+        @pl.when(mine)
+        def _():
+            src, dst = student_copy(t, j, e)
+            inward = pltpu.make_async_copy(src, s_stage, local.at[0])
+            inward.start()
+            inward.wait()
+            outward = pltpu.make_async_copy(s_stage, dst, local.at[0])
+            outward.start()
+            outward.wait()
+
+    other = lax.rem(grp + 1, cores)
+
+    def arrival(t, s):
+        dst = (pq.at[s], pk.at[grp, s], pv.at[grp, s])[t]
+        return send(dst, dst, s_send.at[t, 0, 0], s_recv.at[t, s], other, other)
+
+    def cross(t, s):
+        ref = (None, pk, pv)[t].at[grp, s]
+        return send(ref, ref, x_send.at[t - 1, s], x_recv.at[t - 1, s], blk, other)
+
+    for t in (1, 2, 0):
+        for s in range(cycle):
+            remote = jnp.logical_not((s == blk) & (owner == grp))
+
+            @pl.when(remote)
+            def _():
+                arrival(t, s).wait_recv()
+
+            if t:
+                cross(t, s).start()
+
+    for t in (1, 2):
+        for s in range(cycle):
+            cross(t, s).wait()
+    for copy in int_copies + t_copies:
+        copy.wait()
+    for t, j, e in pieces:
+        mine = (grp * share + j == blk) & (grp == e)
+
+        @pl.when(jnp.logical_not(mine))
+        def _():
+            student_send(t, j, e).wait_send()
+
+
+def arrive(t_query, t_key, t_value, s_query, s_key, s_value, ints, cycle, cores):
+    rows = t_query.shape[0]
+    half = rows // cores
+    share = cycle // cores
+    kind = t_query.dtype
+    any_space = pl.BlockSpec(memory_space=pl.ANY)
+    vmem = pl.BlockSpec(memory_space=pltpu.VMEM)
+    dma = pltpu.SemaphoreType.DMA
+    return pl.pallas_call(
+        functools.partial(arrive_kernel, cycle, cores),
+        in_specs=[any_space] * 6 + [vmem],
+        out_specs=[any_space] * 6 + [vmem],
+        out_shape=[jax.ShapeDtypeStruct((cycle, rows, HD), kind)] * 3
+        + [jax.ShapeDtypeStruct((cycle, half, HD), kind)]
+        + [jax.ShapeDtypeStruct((cores, cycle, half, HD), kind)] * 2
+        + [jax.ShapeDtypeStruct((cycle,) + ints.shape, ints.dtype)],
+        scratch_shapes=[
+            pltpu.VMEM((3, rows, HD), kind),
+            pltpu.VMEM((half, HD), kind),
+            dma((3,)),
+            dma((3, share, cores)),
+            dma((3, cycle)),
+            dma((2, cycle)),
+            dma((2, cycle)),
+            dma((3, cycle - 1)),
+            dma((3, cycle - 1)),
+            dma((cycle - 1,)),
+            dma((cycle - 1,)),
+        ],
+        compiler_params=pltpu.CompilerParams(
+            collective_id=0, has_side_effects=True, vmem_limit_bytes=VMEM_LIMIT
+        ),
+        cost_estimate=pl.CostEstimate(
+            flops=0, bytes_accessed=64 * rows * HD * 2 * cycle, transcendentals=0
+        ),
+    )(t_query, t_key, t_value, s_query, s_key, s_value, ints)
+
+
+def depart_kernel(cycle, cores, dq, own, far, out, got, mine, x_send, x_recv, d_send, d_recv):
+    blk, grp = lax.axis_index("blk"), lax.axis_index("grp")
+    half = dq.shape[1]
+    share = cycle // cores
+    owner, slot = blk // share, lax.rem(blk, share)
+    other = lax.rem(grp + 1, cores)
+    greet(blk, grp, cycle, cores)
+
+    def target(t, j, e):
+        rows = pl.ds(pl.multiple_of(e * half, half), half)
+        return out.at[t, rows, pl.ds(pl.multiple_of(j * HD, HD), HD)]
+
+    def source(t, s):
+        return dq.at[s] if t == 0 else mine.at[t - 1, s]
+
+    def piece(t, s):
+        return send(
+            source(t, s), target(t, slot, grp), d_send.at[t, s], d_recv.at[t, slot, grp], s, owner
+        )
+
+    def local(s):
+        return (s == blk) & (owner == grp)
+
+    def emit(t, s):
+        @pl.when(jnp.logical_not(local(s)))
+        def _():
+            piece(t, s).start()
+
+        @pl.when(local(s))
+        def _():
+            target(t, slot, grp)[...] = source(t, s)[...]
+
+    crossing = [
+        send(far.at[t], got.at[t], x_send.at[t], x_recv.at[t], blk, other) for t in range(2)
+    ]
+    for copy in crossing:
+        copy.start()
+    for s in range(cycle):
+        emit(0, s)
+    for t in range(2):
+        crossing[t].wait_recv()
+        for s in range(cycle):
+            mine[t, s] = (own[t, s] + got[t, s].astype(jnp.float32)).astype(jnp.bfloat16)
+        for s in range(cycle):
+            emit(t + 1, s)
+    for copy in crossing:
+        copy.wait_send()
+    for t in range(3):
+        for j in range(share):
+            for e in range(cores):
+                ours = (grp * share + j == blk) & (grp == e)
+
+                @pl.when(jnp.logical_not(ours))
+                def _():
+                    ref = target(t, j, e)
+                    send(ref, ref, d_send.at[t, 0], d_recv.at[t, j, e], blk, other).wait_recv()
+
+    for t in range(3):
+        for s in range(cycle):
+            @pl.when(jnp.logical_not(local(s)))
+            def _():
+                piece(t, s).wait_send()
+
+
+def depart(dq, own, far, cycle, cores):
+    half = dq.shape[1]
+    share = cycle // cores
+    vmem = pl.BlockSpec(memory_space=pltpu.VMEM)
+    dma = pltpu.SemaphoreType.DMA
+    return pl.pallas_call(
+        functools.partial(depart_kernel, cycle, cores),
+        in_specs=[vmem] * 3,
+        out_specs=vmem,
+        out_shape=jax.ShapeDtypeStruct((3, cores * half, share * HD), jnp.bfloat16),
+        scratch_shapes=[
+            pltpu.VMEM((2, cycle, half, HD), jnp.bfloat16),
+            pltpu.VMEM((2, cycle, half, HD), jnp.bfloat16),
+            dma((2,)),
+            dma((2,)),
+            dma((3, cycle)),
+            dma((3, share, cores)),
+        ],
+        compiler_params=pltpu.CompilerParams(
+            collective_id=1, has_side_effects=True, vmem_limit_bytes=VMEM_LIMIT
+        ),
+    )(dq, own, far)
+
+
+def pair_weights(sel_ref, place_ref, info_ref, per_blk, q_wide, k_all, v_all, k_sel, v_sel):
+    pair = pl.program_id(0)
+    count = sel_ref.shape[1]
+    first_count, grp = info_ref[0], info_ref[1]
+    mine = per_blk // info_ref[2]
+
+    def query_block(index):
+        return (index // mine) * per_blk + grp * mine + lax.rem(index, mine)
+
+    for e in range(count):
+        for h in range(2):
+            source = pl.ds(pl.multiple_of(place_ref[2 * pair + h, e] * BS, BS), BS)
+            cols = slice(h * HD, (h + 1) * HD)
+            k_sel[e * BS : (e + 1) * BS, cols] = k_all[source, :]
+            v_sel[e * BS : (e + 1) * BS, cols] = v_all[source, :]
+    within = lax.broadcasted_iota(jnp.int32, (BS, 1), 0)
+    lane = lax.broadcasted_iota(jnp.int32, (1, 2 * BS), 1)
+    second = lane >= BS
+    query_pos = (
+        jnp.where(second, query_block(2 * pair + 1), query_block(2 * pair)) * BS + lax.rem(lane, BS)
+    )
+    low = jnp.where(query_pos < first_count, 0, first_count)
+    scores = dot(k_sel[...], q_wide[...], NT)
+    allowed = []
+    for e in range(count):
+        base = jnp.where(second, sel_ref[2 * pair + 1, e], sel_ref[2 * pair, e]) * BS
+        allowed.append((within <= query_pos - base) & (within >= low - base))
+    scores = jnp.concatenate(
+        [jnp.where(a, scores[e * BS : (e + 1) * BS], MASKED) for e, a in enumerate(allowed)]
+    )
+    largest = jnp.max(scores, axis=0, keepdims=True)
+    weights = jnp.exp2((scores - largest) * (SCALE * LOG2E))
+    weights = jnp.concatenate(
+        [jnp.where(a, weights[e * BS : (e + 1) * BS], 0.0) for e, a in enumerate(allowed)]
+    )
+    return weights, jnp.sum(weights, axis=0, keepdims=True)
+
+
+def spread_pair(ref, scratch):
+    for h in range(2):
+        scratch[h * BS : (h + 1) * BS, h * HD : (h + 1) * HD] = ref[h * BS : (h + 1) * BS, :].astype(
+            scratch.dtype
+        )
+
+
+def pair_forward_kernel(
+    per_blk, sel_ref, place_ref, info_ref, q_ref, k_all, v_all, o_ref, q_wide, k_sel, v_sel
+):
+    @pl.when(pl.program_id(0) == 0)
+    def _():
+        q_wide[...] = jnp.zeros_like(q_wide)
+
+    spread_pair(q_ref, q_wide)
+    weights, total = pair_weights(
+        sel_ref, place_ref, info_ref, per_blk, q_wide, k_all, v_all, k_sel, v_sel
+    )
+    weights = (weights / total).astype(jnp.bfloat16)
+    blended = dot(weights, v_sel[...], TN)
+    for h in range(2):
+        o_ref[h * BS : (h + 1) * BS, :] = blended[
+            h * BS : (h + 1) * BS, h * HD : (h + 1) * HD
+        ].astype(jnp.bfloat16)
+
+
+def pair_backward_kernel(
+    per_blk, sel_ref, place_ref, info_ref, q_ref, g_ref, k_all, v_all, dq_ref, own_ref, far_ref,
+    dk_sum, dv_sum, q_wide, g_wide, k_sel, v_sel,
+):
+    pair = pl.program_id(0)
+
+    @pl.when(pair == 0)
+    def _():
+        q_wide[...] = jnp.zeros_like(q_wide)
+        g_wide[...] = jnp.zeros_like(g_wide)
+        dk_sum[...] = jnp.zeros_like(dk_sum)
+        dv_sum[...] = jnp.zeros_like(dv_sum)
+
+    spread_pair(q_ref, q_wide)
+    spread_pair(g_ref, g_wide)
+    weights, total = pair_weights(
+        sel_ref, place_ref, info_ref, per_blk, q_wide, k_all, v_all, k_sel, v_sel
+    )
+    weights = weights / total
+    weight_grad = dot(v_sel[...], g_wide[...], NT)
+    row_dots = jnp.sum(weights * weight_grad, axis=0, keepdims=True)
+    score_grad = (weights * (weight_grad - row_dots) * SCALE).astype(jnp.bfloat16)
+    query_grad = dot(score_grad, k_sel[...], TN)
+    for h in range(2):
+        dq_ref[h * BS : (h + 1) * BS, :] = query_grad[
+            h * BS : (h + 1) * BS, h * HD : (h + 1) * HD
+        ].astype(jnp.bfloat16)
+    key_grad = dot(score_grad, q_wide[...])
+    value_grad = dot(weights.astype(jnp.bfloat16), g_wide[...])
+    for e in range(sel_ref.shape[1]):
+        for h in range(2):
+            target = pl.ds(pl.multiple_of(place_ref[2 * pair + h, e] * BS, BS), BS)
+            cols = slice(h * HD, (h + 1) * HD)
+            dk_sum[target, :] += key_grad[e * BS : (e + 1) * BS, cols]
+            dv_sum[target, :] += value_grad[e * BS : (e + 1) * BS, cols]
+
+    @pl.when(pair == pl.num_programs(0) - 1)
+    def _():
+        part = own_ref.shape[1]
+        near = pl.ds(pl.multiple_of(info_ref[1] * part, part), part)
+        away = pl.ds(pl.multiple_of((info_ref[2] - 1 - info_ref[1]) * part, part), part)
+        own_ref[0] = dk_sum[near, :]
+        own_ref[1] = dv_sum[near, :]
+        far_ref[0] = dk_sum[away, :].astype(jnp.bfloat16)
+        far_ref[1] = dv_sum[away, :].astype(jnp.bfloat16)
+
+
+def pair_scratch(keys, wides):
+    return [pltpu.VMEM((2 * BS, 2 * HD), jnp.bfloat16)] * wides + [
+        pltpu.VMEM((keys, 2 * HD), jnp.bfloat16),
+        pltpu.VMEM((keys, 2 * HD), jnp.bfloat16),
+    ]
+
+
+def pair_forward(per_blk, tables, queries, keys, values):
+    rows, width = queries.shape
+    tokens = keys.shape[0]
+    row_block = pl.BlockSpec((2 * BS, width), lambda b, *_: (b, 0))
+    whole = pl.BlockSpec((tokens, width), lambda b, *_: (0, 0))
+    return pl.pallas_call(
+        functools.partial(pair_forward_kernel, per_blk),
+        grid_spec=pltpu.PrefetchScalarGridSpec(
+            num_scalar_prefetch=3,
+            grid=(rows // (2 * BS),),
+            in_specs=[row_block, whole, whole],
+            out_specs=row_block,
+            scratch_shapes=pair_scratch(tables[0].shape[1] * BS, 1),
+        ),
+        out_shape=jax.ShapeDtypeStruct((rows, width), jnp.bfloat16),
+        compiler_params=pltpu.CompilerParams(vmem_limit_bytes=VMEM_LIMIT),
+        cost_estimate=pl.CostEstimate(
+            flops=16 * rows * tokens * width, bytes_accessed=4 * tokens * width, transcendentals=0
+        ),
+    )(*tables, queries, keys, values)
+
+
+def pair_backward(per_blk, cores, tables, queries, grads, keys, values):
+    rows, width = queries.shape
+    tokens = keys.shape[0]
+    part = tokens // cores
+    row_block = pl.BlockSpec((2 * BS, width), lambda b, *_: (b, 0))
+    whole = pl.BlockSpec((tokens, width), lambda b, *_: (0, 0))
+    both = pl.BlockSpec((2, part, width), lambda b, *_: (0, 0, 0))
+    return pl.pallas_call(
+        functools.partial(pair_backward_kernel, per_blk),
+        grid_spec=pltpu.PrefetchScalarGridSpec(
+            num_scalar_prefetch=3,
+            grid=(rows // (2 * BS),),
+            in_specs=[row_block, row_block, whole, whole],
+            out_specs=[row_block, both, both],
+            scratch_shapes=[pltpu.VMEM((tokens, width), jnp.float32)] * 2
+            + pair_scratch(tables[0].shape[1] * BS, 2),
+        ),
+        out_shape=[
+            jax.ShapeDtypeStruct((rows, width), jnp.bfloat16),
+            jax.ShapeDtypeStruct((2, part, width), jnp.float32),
+            jax.ShapeDtypeStruct((2, part, width), jnp.bfloat16),
+        ],
+        compiler_params=pltpu.CompilerParams(vmem_limit_bytes=VMEM_LIMIT),
+        cost_estimate=pl.CostEstimate(
+            flops=32 * rows * tokens * width, bytes_accessed=8 * tokens * width, transcendentals=0
+        ),
+    )(*tables, queries, grads, keys, values)
+
+
+def heads_on_chips(
+    t_query, t_key, t_value, t_out, s_query, s_key, s_value, s_out, segments, selection
+):
+    rows = t_query.shape[0]
+    cycle, cores = lax.axis_size("blk"), lax.axis_size("grp")
+    split = ("head", "grp")
+    groups = lax.axis_size("head") * cores
+    blk, grp = lax.axis_index("blk"), lax.axis_index("grp")
+    half = rows // cores
+    share = cycle // cores
+    per_blk = rows // BS
+    mine = per_blk // cores
+    picks = selection.shape[1]
+
+    piece = s_out.shape[0] // cycle
+    s_rows = lax.dynamic_slice_in_dim(s_out, blk * piece, piece, 0)
+    s_rows = lax.all_gather(s_rows, split, axis=0, tiled=True)
+
+    lanes = 128
+    ints = jnp.concatenate(
+        [segments.reshape(rows // lanes, lanes), jnp.pad(selection, ((0, 0), (0, lanes - picks)))]
+    )
+    tq, tk, tv, pq, pk, pv, ints = arrive(
+        t_query, t_key, t_value, s_query, s_key, s_value, ints, cycle, cores
+    )
+    s_rows, tq = lax.optimization_barrier((s_rows, tq))
+    seg_rows = rows // lanes
+    first_count = jnp.sum((ints[:, :seg_rows] == 0).astype(jnp.int32))
+    info = jnp.stack([first_count, grp, jnp.int32(cores)]).astype(jnp.int32)
+    chosen = lax.dynamic_slice_in_dim(ints[:, seg_rows:, :picks], grp * mine, mine, 1)
+    chosen = chosen.reshape(cycle * mine, picks)
+    at = chosen % per_blk
+    place = ((at // mine) * cycle + chosen // per_blk) * mine + at % mine
+    tables = (chosen, place, info)
+    pq = pq.reshape(cycle * half, HD)
+    pk, pv = pk.reshape(cycle * rows, HD), pv.reshape(cycle * rows, HD)
+
+    blended = pair_forward(per_blk, tables, pq, pk, pv)
+    tables, blended, tq = lax.optimization_barrier((tables, blended, tq))
+    blended = lax.all_to_all(blended.reshape(cycle, half, HD), "blk", 0, 0, tiled=True)
+    blended = lax.all_to_all(blended, "grp", split_axis=0, concat_axis=1, tiled=True)
+    s_attn = blended.transpose(1, 0, 2).reshape(rows, share * HD)
+
+    mix = jnp.concatenate([dot(s_rows, t_out, NT), dot(s_rows, s_out, NT)], axis=1)
+    mix = lax.all_gather(mix.astype(jnp.bfloat16), "blk")
+
+    whole = [x.reshape(cycle * rows, HD) for x in (tq, tk, tv)]
+    whole_heads = teacher(*whole, 1, (1, (0, 0, 0)), jnp.int32(0), first_count)
+    t_attn = lax.all_to_all(whole_heads, "blk", split_axis=0, concat_axis=1, tiled=True)
+
+    grad_terms = project_grads(s_attn, t_attn, mix, groups)
+    grads = lax.psum_scatter(grad_terms, split, scatter_dimension=0, tiled=False)
+    terms = project(s_attn, t_attn, s_out, t_out, groups)
+    terms, grads = lax.optimization_barrier((terms, grads))
+    mismatch = lax.psum_scatter(terms, split, scatter_dimension=0, tiled=False)
+
+    grads = grads.reshape(rows, share, HD).transpose(1, 0, 2)
+    grads = lax.all_to_all(grads, "grp", split_axis=1, concat_axis=0, tiled=True)
+    grads = lax.all_to_all(grads, "blk", 0, 0, tiled=True).reshape(cycle * half, HD)
+    dq, own, far = pair_backward(per_blk, cores, tables, pq, grads, pk, pv)
+    out = depart(
+        dq.reshape(cycle, half, HD),
+        own.reshape(2, cycle, half, HD),
+        far.reshape(2, cycle, half, HD),
+        cycle,
+        cores,
+    ).astype(jnp.float32)
+    return (mismatch.astype(jnp.float32), out[0], out[1], out[2])
+
+
 def on_device(t_query, t_key, t_value, t_out, s_query, s_key, s_value, s_out, segments, selection):
     row_count = t_query.shape[0]
     heads = t_query.shape[1] // HD
     cycle = lax.axis_size("blk")
     split = ("head", "grp")
     groups = lax.axis_size("head") * lax.axis_size("grp")
+    cores = lax.axis_size("grp")
+    if cores == 2 and heads == cycle and s_query.shape[1] // HD * cores == cycle:
+        return heads_on_chips(
+            t_query, t_key, t_value, t_out, s_query, s_key, s_value, s_out, segments, selection
+        )
     my_index = lax.axis_index("blk")
     first_row = my_index * row_count
     shard_blocks = row_count // BS

time: 341 us -> 316 us (0.927)
  waiting for transfers between devices: 163 us -> 70.1 us
  Pallas kernels: 94.8 us -> 177 us
  starting transfers between devices: 32.3 us -> 7.87 us
  blocking collectives: 0 us -> 20.7 us
  local copies, waits for them, and re-layouts: 15 us -> 8.64 us
    pallas_call x2 -> x4, Pallas kernels: 47.1 us -> 126 us  [the longest x1 58.9 us: arrive(): pl.pallas_call(functools.partial(arrive_kernel, cycle, cores), in_specs=[...]
    ppermute x12 -> x0, waiting for transfers between devices: 72.9 us -> none  [the longest x3 45.9 us: on_device(): lax.ppermute(far[distance - 1], 'blk', route).astype(jnp.float32)]
    all_gather x2, waiting for transfers between devices: 42.4 us -> 0.02 us  [the longest x1 0.02 us: heads_on_chips(): s_rows = lax.all_gather(s_rows, split, axis=0, tiled=True)]
    ppermute x12 -> x0, starting transfers between devices: 23.2 us -> none  [the longest x6 15.8 us: from_earlier(): return lax.ppermute(rows, 'blk', route)]
    all_to_all x0 -> x3, blocking collectives: none -> 20.7 us  [the longest x1 12.4 us: heads_on_chips(): lax.all_to_all(grads, 'blk', 0, 0, tiled=True).reshape(cycle * half, HD)]
    all_to_all x2, waiting for transfers between devices: 0.01 us -> 12.5 us  [the longest x1 12.5 us: heads_on_chips(): lax.all_to_all(whole_heads, 'blk', split_axis=0, concat_axis=1, tiled=True)]
    reduce_scatter x2, waiting for transfers between devices: 47.9 us -> 57.5 us  [the longest x1 38 us: heads_on_chips(): lax.psum_scatter(grad_terms, split, scatter_dimension=0, tiled=False)]
    unnamed x30 -> x9, local copies, waits for them, and re-layouts: 7.88 us -> 1.91 us
  transfers between devices with their start and end apart: 18 -> 6, of which waited for: 8 -> 3; matrix products, arithmetic and copies ran while one was open for 8% -> 4% of each run, Pallas kernels for 25% -> 53%
where the time goes in v2:
time: 316 us
  Pallas kernels  177 us (56%)
  waiting for transfers between devices  70.1 us (22%)
  blocking collectives  20.7 us (7%)
  between operations  13.9 us (4%)
  other arithmetic  9.62 us (3%)
  local copies, waits for them, and re-layouts  8.64 us (3%)
  matrix products  8.37 us (3%)
  starting transfers between devices  7.87 us (2%)
    pallas_call x1, Pallas kernels, arrive(): pl.pallas_call(functools.partial(arrive_kernel, cycle, cores), in_specs=[...  58.9 us
    reduce_scatter x1, waiting for transfers between devices, heads_on_chips(): lax.psum_scatter(grad_terms, split, scatter_dimension=0, tiled=False)  38 us
    pallas_call x1, Pallas kernels, teacher(): pl.pallas_call(functools.partial(teacher_kernel, tile), grid_spec=pltpu.P...  29.3 us
    pallas_call x1, Pallas kernels, pair_backward(): pl.pallas_call(functools.partial(pair_backward_kernel, per_blk), grid_spe...  27.5 us
    pallas_call x1, Pallas kernels, depart(): pl.pallas_call(functools.partial(depart_kernel, cycle, cores), in_specs=[...  21.8 us
    reduce_scatter x1, waiting for transfers between devices, heads_on_chips(): mismatch = lax.psum_scatter(terms, split, scatter_dimension=0, tiled=False)  19.5 us
    pallas_call x1, Pallas kernels, pair_forward(): pl.pallas_call(functools.partial(pair_forward_kernel, per_blk), grid_spec...  18.1 us
    all_to_all x1, waiting for transfers between devices, heads_on_chips(): lax.all_to_all(whole_heads, 'blk', split_axis=0, concat_axis=1, tiled=True)  12.5 us
  transfers between devices with their start and end apart: 6, of which 3 were waited for; matrix products, arithmetic and copies ran while one was open for 4% of the time, Pallas kernels for 53%

profile of v2, /device:TPU:0, one launch (start us, length us, event | category | flops | bytes accessed | tf_op | source)
XLA Modules:
  0.0 316.1 jit_solution(16084445734178873548)
XLA Ops:
  7.2 0.0 all-gather.3.cloned.1.call-start
  7.2 0.0 copy-start.1
  7.2 2.0 constant_dynamic-slice_fusion
  9.2 0.0 all-gather.3.cloned.1.call-update
  9.3 0.0 all-gather.5.cloned.1.call-start
  9.3 1.3 pad_add_fusion.ints
  10.6 58.9 %shard_map.129 = (bf16[4,1024,128]{2,1,0:T(8,128)(2,1)}, bf16[4,1024,128]{2,1,0:T(8,128)(2,1)}, bf16[4,1024,128]{2,1,0:T(8,128)(2,1)}, bf16[4,512,128]{2,1,0:T(8...) custom-call(bf16[1024,512]{1,0:T(8,128)(2,1)} %tq.1, ...), custom_call_target="tpu_custom_call" | custom-call | bytes 67108864 | tf_op jit(solution)/shard_map/pallas_call | solution.py:450
  69.5 0.0 all-gather.3.cloned.1.call-done
  69.5 0.0 copy-done.1
  69.6 0.0 copy-start
  69.6 3.6 %fusion.1 = bf16[1,512,256]{1,2,0:T(8,128)(2,1)S(1)} fusion(bf16[512,4096]{1,0:T(8,128)(2,1)} %all-gather.3.cloned.1.call-done, bf16[256,4096]{1,0:T(8,128)(2,1)S(1)} %copy-done.1), kind=kOutput, calls=%fused_computation.3 | convolution fusion | flops 1073872896 | bytes 6553600 | tf_op jit(solution)/shard_map/dot_general | solution.py:22
  73.2 0.0 copy-done
  73.2 4.7 %fusion = bf16[1,512,512]{1,2,0:T(8,128)(2,1)S(1)} fusion(bf16[512,4096]{1,0:T(8,128)(2,1)} %all-gather.3.cloned.1.call-done, bf16[512,4096]{1,0:T(8,128)(2,1)S(1)} %copy-done), kind=kOutput, calls=%fused_computation.1 | convolution fusion | flops 2147745792 | bytes 8912896 | tf_op jit(solution)/shard_map/dot_general | solution.py:22
  78.0 0.0 copy-start.3
  78.0 0.1 pad_maximum_fusion
  78.0 1.2 copy.21
  79.2 0.0 all-gather.5.cloned.1.call-update
  79.2 0.6 convert_reduce_fusion
  79.9 1.2 pad_add_fusion.2.info_ref
  81.1 1.2 pad_add_fusion.1.info_ref
  82.3 0.6 fusion.5
  82.9 18.1 %shard_map.130 = bf16[2048,128]{1,0:T(8,128)(2,1)} custom-call(s32[32,16]{1,0:T(8,128)} %get-tuple-element.35.sel_ref, s32[32,16]{1,0:T(8,128)} %get-tuple-element.36.place_ref, s32[3]{0:T(128)} %pad_add_fusion.1.info_ref, bf16[2048,128]{1,0:T(8,128)(2,1)} %bitcast.79, bf16[4096,128]{1,0:T(8,128)(2,1)} %bitcast.72, bf16[4096,128]{1,0:T(8,128)(2,1)} %bitcast.74), custom_call_target="tpu_custom_call" | custom-call | flops 17179869184 | bytes 2097152 | tf_op jit(solution)/shard_map/pallas_call | solution.py:691
  101.0 3.6 %all-to-all-start = ((bf16[4,512,128]{2,1,0:T(8,128)(2,1)}), bf16[4,512,128]{2,1,0:T(8,128)(2,1)S(1)}, u32[]{:S(2)}, u32[]{:S(2)}) async-start(bf16[4,512,128]{2,1,0:T(8,128)(2,1)} %bitcast.69), calls=%async_computation | async-start | bytes 1048576 | tf_op jit(solution)/shard_map/all_to_all | solution.py:776
  104.6 29.3 %shard_map.131 = bf16[4096,128]{1,0:T(8,128)(2,1)} custom-call(s32[2]{0:T(128)} %pad_add_fusion.2.info_ref, bf16[4096,128]{1,0:T(8,128)(2,1)} %bitcast.76, bf16[4096,128]{1,0:T(8,128)(2,1)} %bitcast.77, bf16[4096,128]{1,0:T(8,128)(2,1)} %bitcast.78), custom_call_target="tpu_custom_call" | custom-call | flops 4294967296 | bytes 4194304 | tf_op jit(solution)/shard_map/pallas_call | solution.py:83
  133.9 0.0 all-to-all-done
  133.9 4.1 %all_to_all.65 = bf16[4,512,128]{2,1,0:T(8,128)(2,1)S(1)} all-to-all(bf16[4,512,128]{2,1,0:T(8,128)(2,1)S(1)} %all-to-all-done), channel_id=1, replica_groups=mesh['blk'=4,'head'=4,'grp'=2] {'grp'}, dimensions={0} | all-to-all | bytes 1048576 | tf_op jit(solution)/shard_map/all_to_all | solution.py:777
  138.1 4.1 %all-to-all-start.2 = ((bf16[4,1024,128]{2,1,0:T(8,128)(2,1)}), bf16[4,1024,128]{2,1,0:T(8,128)(2,1)S(1)}, u32[]{:S(2)}, u32[]{:S(2)}) async-start(bf16[4,1024,128]{2,1,0:T(8,128)(2,1)} %bitcast.66), calls=%async_computation.2 | async-start | bytes 2097152 | tf_op jit(solution)/shard_map/all_to_all | solution.py:785
  142.2 0.5 copy.19
  142.7 0.9 copy.27
  143.6 12.5 %all-to-all-done.2 = bf16[4,1024,128]{2,1,0:T(8,128)(2,1)S(1)} async-done(((bf16[4,1024,128]{2,1,0:T(8,128)(2,1)}), bf16[4,1024,128]{2,1,0:T(8,128)(2,1)S(1)}, u32[]{:S(2)}, u32[]{:S(2)}) %all-to-all-start.2) | async-done | bytes 1048608 | tf_op jit(solution)/shard_map/all_to_all | solution.py:785
  156.1 1.1 copy_bitcast_fusion.t_attn
  157.2 9.0 %shard_map.133 = bf16[8,1024,256]{2,1,0:T(8,128)(2,1)} custom-call(bf16[1024,256]{1,0:T(8,128)(2,1)} %bitcast.57, bf16[1024,512]{1,0:T(8,128)(2,1)} %copy_bitcast_fusion.t_attn, bf16[4,512,768]{2,1,0:T(8,128)(2,1)} %all-gather.5.cloned.1.call-done.mix), custom_call_target="tpu_custom_call" | custom-call | tf_op jit(solution)/shard_map/pallas_call | solution.py:288
  166.2 0.0 reduce-scatter.3.cloned.1.call-update
  166.3 0.0 reduce-scatter.5.cloned.1.call-start
  166.3 12.3 %shard_map.132 = bf16[8,1024,512]{2,1,0:T(8,128)(2,1)} custom-call(bf16[1024,256]{1,0:T(8,128)(2,1)} %bitcast.58, bf16[1024,512]{1,0:T(8,128)(2,1)} %copy_bitcast_fusion.t_attn, bf16[256,4096]{1,0:T(8,128)(2,1)} %s_out.1, bf16[512,4096]{1,0:T(8,128)(2,1)} %t_out.1), custom_call_target="tpu_custom_call" | custom-call | tf_op jit(solution)/shard_map/pallas_call | solution.py:261
  178.6 38.0 %reduce-scatter.3.cloned.1.call-done = bf16[1,1024,256]{2,1,0:T(8,128)(2,1)} async-done(((bf16[8,1024,256]{2,1,0:T(8,128)(2,1)}), bf16[1,1024,256]{2,1,0:T(8,128)(2,1)}) %reduce-scatter.3.cloned.1.call-update) | async-done | bytes 524304 | tf_op jit(solution)/shard_map/reduce_scatter | solution.py:788
  216.6 0.0 reduce-scatter.5.cloned.1.call-update
  216.6 1.0 copy-done.2
  217.6 0.1 reshape.99
  217.8 4.2 %all_to_all.66 = bf16[2,1024,128]{2,0,1:T(2,128)(2,1)S(1)} all-to-all(bf16[2,1024,128]{2,0,1:T(2,128)(2,1)S(1)} %bitcast.62), channel_id=1, replica_groups=mesh['blk'=4,'head'=4,'grp'=2] {'grp'}, dimensions={1} | all-to-all | bytes 1048576 | tf_op jit(solution)/shard_map/all_to_all | solution.py:794
  221.9 0.1 copy.22
  222.0 12.4 %all_to_all.67 = bf16[4,512,128]{2,1,0:T(8,128)(2,1)} all-to-all(bf16[4,512,128]{2,1,0:T(8,128)(2,1)S(1)} %bitcast.64), channel_id=1, replica_groups=mesh['blk'=4,'head'=4,'grp'=2] {'blk'}, dimensions={0} | all-to-all | bytes 1048576 | tf_op jit(solution)/shard_map/all_to_all | solution.py:795
  234.4 27.5 %shard_map.134 = (bf16[2048,128]{1,0:T(8,128)(2,1)}, f32[2,2048,128]{2,1,0:T(8,128)}, bf16[2,2048,128]{2,1,0:T(8,128)(2,1)}) custom-call(s32[32,16]{1,0:T(8,128)} %get-tuple-element.35.sel_ref, s32[32,16]{1,0:T(8,128)} %get-tuple-element.36.place_ref, s32[3]{0:T(128)} %pad_add_fusion.1.info_ref, bf16[2048,128]{1,0:T(8,128)(2,1)} %bitcast.80, ...), custom_call_target="tpu_custom_call" | custom-call | flops 34359738368 | bytes 4194304 | tf_op jit(solution)/shard_map/pallas_call | solution.py:715
  261.9 21.8 %shard_map.135 = bf16[3,1024,256]{2,1,0:T(8,128)(2,1)} custom-call(bf16[4,512,128]{2,1,0:T(8,128)(2,1)} %bitcast.67, f32[2,4,512,128]{3,2,1,0:T(8,128)} %bitcast.59, bf16[2,4,512,128]{3,2,1,0:T(8,128)(2,1)} %bitcast.65), custom_call_target="tpu_custom_call" | custom-call | tf_op jit(solution)/shard_map/pallas_call | solution.py:549
  283.8 1.7 convert_element_type.23
  285.5 1.7 slice_bitcast_fusion
  287.2 19.5 %reduce-scatter.5.cloned.1.call-done = bf16[1,1024,512]{2,1,0:T(8,128)(2,1)} async-done(((bf16[8,1024,512]{2,1,0:T(8,128)(2,1)}), bf16[1,1024,512]{2,1,0:T(8,128)(2,1)}) %reduce-scatter.5.cloned.1.call-update) | async-done | bytes 1048592 | tf_op jit(solution)/shard_map/reduce_scatter | solution.py:791
  306.8 2.8 bitcast_convert_fusion
  (5 shorter events, 0.0 us)
Async XLA Ops:
  7.2 62.4 %all-gather.3.cloned.1.call-start = ((), (), s32[]{:S(2)}) async-start(), calls=%async_computation.7 | async-start | bytes 4718592 | tf_op jit(solution)/shard_map/all_gather | solution.py:753
  7.2 62.3 %copy-start.1 = (bf16[256,4096]{1,0:T(8,128)(2,1)S(1)}, bf16[256,4096]{1,0:T(8,128)(2,1)}, u32[]{:S(2)}) copy-start(bf16[256,4096]{1,0:T(8,128)(2,1)} %s_out.1) | copy-start | bytes 6291460
  9.3 147.9 %all-gather.5.cloned.1.call-start = ((), (), s32[]{:S(2)}) async-start(), calls=%async_computation.8 | async-start | bytes 3932160 | tf_op jit(solution)/shard_map/all_gather | solution.py:781
  69.6 3.6 %copy-start = (bf16[512,4096]{1,0:T(8,128)(2,1)S(1)}, bf16[512,4096]{1,0:T(8,128)(2,1)}, u32[]{:S(2)}) copy-start(bf16[512,4096]{1,0:T(8,128)(2,1)} %t_out.1) | copy-start | bytes 12582916
  78.0 1.3 copy-start.3
  101.0 32.9 %all-to-all-start = ((bf16[4,512,128]{2,1,0:T(8,128)(2,1)}), bf16[4,512,128]{2,1,0:T(8,128)(2,1)S(1)}, u32[]{:S(2)}, u32[]{:S(2)}) async-start(bf16[4,512,128]{2,1,0:T(8,128)(2,1)} %bitcast.69), calls=%async_computation | async-start | bytes 1048576 | tf_op jit(solution)/shard_map/all_to_all | solution.py:776
  138.1 18.1 %all-to-all-start.2 = ((bf16[4,1024,128]{2,1,0:T(8,128)(2,1)}), bf16[4,1024,128]{2,1,0:T(8,128)(2,1)S(1)}, u32[]{:S(2)}, u32[]{:S(2)}) async-start(bf16[4,1024,128]{2,1,0:T(8,128)(2,1)} %bitcast.66), calls=%async_computation.2 | async-start | bytes 2097152 | tf_op jit(solution)/shard_map/all_to_all | solution.py:785
  142.2 74.4 %reduce-scatter.3.cloned.1.call-start = ((), (), s32[]{:S(2)}) async-start(), calls=%async_computation.9 | async-start | bytes 4718592 | tf_op jit(solution)/shard_map/reduce_scatter | solution.py:788
  166.3 140.5 %reduce-scatter.5.cloned.1.call-start = ((), (), s32[]{:S(2)}) async-start(), calls=%async_computation.10 | async-start | bytes 9437184 | tf_op jit(solution)/shard_map/reduce_scatter | solution.py:791
  216.6 1.0 copy-start.2
Sparse Core Ops, SparseCore 0:
  10.1 49.5 all-gather.2
  79.3 50.1 all-gather.4
  166.4 50.1 reduce-scatter.2
  218.8 87.9 reduce-scatter.4

commit v3 on v2

--- a/solution.py
+++ b/solution.py
@@ -734,6 +734,348 @@
     )(*tables, queries, grads, keys, values)
 
 
+def combine_kernel(
+    cycle, cores, line, chunks, kept, heads_t, heads_s, mix_hbm, t_hbm, s_hbm,
+    g_out, m_out, terms,
+    mix, t_w, s_w, t_attn, s_attn, g_own, g_far, g_got, g_line, m_own, m_far, m_got, m_line,
+    total, g_done, w_sem, t_send, t_recv, t_local, s_send, s_recv, s_local,
+    gx_send, gx_recv, gz_send, gz_recv, mx_send, mx_recv, mz_send, mz_recv, d_send, d_recv,
+):
+    blk, grp, pos = lax.axis_index("blk"), lax.axis_index("grp"), lax.axis_index("head")
+    share = cycle // cores
+    owner, slot = blk // share, lax.rem(blk, share)
+    other = lax.rem(grp + 1, cores)
+    step = t_attn.shape[0] // chunks
+    per_half = chunks // cores
+
+    loads = [
+        pltpu.make_async_copy(src, dst, w_sem.at[n])
+        for n, (src, dst) in enumerate(((mix_hbm, mix), (t_hbm, t_w), (s_hbm, s_w)))
+    ]
+    for load in loads:
+        load.start()
+
+    barrier = pltpu.get_barrier_semaphore()
+    for d in range(cycle):
+        for e in range(cores):
+            if d or e:
+                pl.semaphore_signal(
+                    barrier,
+                    inc=1,
+                    device_id={"blk": lax.rem(blk + d, cycle), "grp": lax.rem(grp + e, cores)},
+                    device_id_type=MESH,
+                )
+    for ahead, there in ((-1, pos > 0), (1, pos < line - 1)):
+        @pl.when(there)
+        def _():
+            pl.semaphore_signal(
+                barrier, inc=1, device_id={"head": pos + ahead}, device_id_type=MESH
+            )
+
+    ends = jnp.where(pos > 0, 1, 0) + jnp.where(pos < line - 1, 1, 0)
+    pl.semaphore_wait(barrier, cycle * cores - 1 + ends)
+
+    def t_copy(i, d):
+        dest = lax.rem(blk + d, cycle)
+        src = heads_t.at[dest, pl.ds(i * step, step), :]
+        dst = t_attn.at[pl.ds(i * step, step), pl.ds(pl.multiple_of(blk * HD, HD), HD)]
+        if d == 0:
+            return pltpu.make_async_copy(src, dst, t_local.at[i])
+        return send(src, dst, t_send.at[i, d - 1], t_recv.at[i, d - 1], dest, grp)
+
+    def s_ends(r, s):
+        rows = pl.ds(pl.multiple_of((grp * per_half + r) * step, step), step)
+        dst = s_attn.at[rows, pl.ds(pl.multiple_of(slot * HD, HD), HD)]
+        return heads_s.at[s, pl.ds(r * step, step), :], dst
+
+    def s_copy(r, s):
+        return send(
+            *s_ends(r, s), s_send.at[r, s], s_recv.at[slot, grp * per_half + r], s, owner
+        )
+
+    def s_here(r, s):
+        return pltpu.make_async_copy(*s_ends(r, s), s_local.at[r])
+
+    for i in range(chunks):
+        for d in range(cycle):
+            t_copy(i, d).start()
+        if i < per_half:
+            for s in range(cycle):
+                here = (s == blk) & (owner == grp)
+
+                @pl.when(here)
+                def _():
+                    s_here(i, s).start()
+
+                @pl.when(jnp.logical_not(here))
+                def _():
+                    s_copy(i, s).start()
+
+    def await_inputs(i):
+        for d in range(1, cycle):
+            t_copy(i, d).wait_recv()
+        t_copy(i, 0).wait()
+        e, r = i // per_half, i % per_half
+        for j in range(share):
+            here = (grp * share + j == blk) & (grp == e)
+
+            @pl.when(here)
+            def _():
+                s_here(r, grp * share + j).wait()
+
+            @pl.when(jnp.logical_not(here))
+            def _():
+                ref = s_attn.at[pl.ds(i * step, step), pl.ds(j * HD, HD)]
+                send(ref, ref, s_send.at[r, 0], s_recv.at[j, i], blk, other).wait_recv()
+
+    t_width, s_width = t_attn.shape[1], s_attn.shape[1]
+
+    def rows_of(i):
+        rows = pl.ds(i * step, step)
+        return t_attn[rows, :], s_attn[rows, :]
+
+    def grad_term(i, group):
+        t_rows, s_rows = rows_of(i)
+        depth = mix.shape[1] // (line * cores)
+        part = mix[:, pl.ds(pl.multiple_of(group * depth, depth), depth), :]
+        part = part.reshape(mix.shape[0] * depth, mix.shape[2])
+        value = dot(s_rows, part[:, t_width:], NT) - dot(t_rows, part[:, :t_width], NT)
+        return value.astype(jnp.bfloat16)
+
+    def out_term(i, group):
+        t_rows, s_rows = rows_of(i)
+        width = t_w.shape[1] // (line * cores)
+        cols = pl.ds(pl.multiple_of(group * width, width), width)
+        return (dot(s_rows, s_w[:, cols]) - dot(t_rows, t_w[:, cols])).astype(jnp.bfloat16)
+
+    kinds = {
+        "g": (grad_term, g_own, g_far, g_got, g_line, gx_send, gx_recv, gz_send, gz_recv),
+        "m": (out_term, m_own, m_far, m_got, m_line, mx_send, mx_recv, mz_send, mz_recv),
+    }
+
+    def cross(kind, i):
+        _, _, far, got, _, x_send, x_recv, _, _ = kinds[kind]
+        return send(far.at[i], got.at[i], x_send.at[i], x_recv.at[i], blk, other)
+
+    def hop(kind, i, way, dest, target):
+        _, own, _, _, relay, _, _, z_send, z_recv = kinds[kind]
+        return pltpu.make_async_remote_copy(
+            src_ref=own.at[i, dest],
+            dst_ref=relay.at[way, i, dest],
+            send_sem=z_send.at[i, dest],
+            recv_sem=z_recv.at[way, i, dest],
+            device_id={"head": target},
+            device_id_type=MESH,
+        )
+
+    def compute(kind, i):
+        if kind == "g":
+            await_inputs(i)
+        if (kind, i) == ("g", 0):
+            loads[0].wait()
+        if (kind, i) == ("m", 0):
+            loads[1].wait()
+            loads[2].wait()
+        term, own, far = kinds[kind][:3]
+
+        def body(z, carry):
+            far[i, z] = term(i, z * cores + other)
+            own[i, z] = term(i, z * cores + grp)
+            return carry
+
+        lax.fori_loop(0, line, body, 0)
+        cross(kind, i).start()
+
+    def add(kind, i, dest, ref):
+        own = kinds[kind][1]
+        own[i, dest] = (
+            own[i, dest].astype(jnp.float32) + ref[...].astype(jnp.float32)
+        ).astype(jnp.bfloat16)
+
+    def fold(kind, i):
+        got = kinds[kind][3]
+        cross(kind, i).wait_recv()
+
+        def body(z, carry):
+            add(kind, i, z, got.at[i, z])
+            return carry
+
+        lax.fori_loop(0, line, body, 0)
+
+    def flow(kind, i, upward):
+        way = jnp.where(upward, 0, 1)
+        target = jnp.where(upward, pos + 1, pos - 1)
+        count = jnp.where(upward, line - 1 - pos, pos)
+        fed = jnp.where(upward, pos, line - 1 - pos) > 0
+        relay = kinds[kind][4]
+
+        def body(k, carry):
+            dest = jnp.where(upward, line - 1 - k, k)
+
+            @pl.when(fed)
+            def _():
+                hop(kind, i, way, dest, target).wait_recv()
+                add(kind, i, dest, relay.at[way, i, dest])
+
+            hop(kind, i, way, dest, target).start()
+            return carry
+
+        lax.fori_loop(0, count, body, 0)
+
+    def final(kind, i):
+        own, relay = kinds[kind][1], kinds[kind][4]
+        width = own.shape[3]
+        total[:, :width] = own[i, pos].astype(jnp.float32)
+        for way, fed in ((0, pos > 0), (1, pos < line - 1)):
+            @pl.when(fed)
+            def _():
+                hop(kind, i, way, pos, pos).wait_recv()
+                total[:, :width] += relay[way, i, pos].astype(jnp.float32)
+
+        if kind == "m":
+            m_out[pl.ds(i * step, step), :] = total[...]
+            return
+        for j in range(share):
+            g_done[i, j] = total[:, j * HD : (j + 1) * HD].astype(jnp.bfloat16)
+            here = (grp * share + j == blk) & (grp == i // per_half)
+
+            @pl.when(here)
+            def _():
+                g_out[blk, pl.ds(i % per_half * step, step), :] = g_done[i, j]
+
+            @pl.when(jnp.logical_not(here))
+            def _():
+                deliver(i, j).start()
+
+    def deliver(i, j):
+        r = i % per_half
+        return send(
+            g_done.at[i, j],
+            g_out.at[blk, pl.ds(r * step, step), :],
+            d_send.at[i, j],
+            d_recv.at[blk, r],
+            grp * share + j,
+            i // per_half,
+        )
+
+    low = pos < line // 2
+    items = [("g", i) for i in range(chunks)] + [("m", i) for i in range(kept)]
+    for k in range(len(items) + 3):
+        if k < len(items):
+            compute(*items[k])
+        if k == len(items) and kept < chunks:
+            if not kept:
+                loads[1].wait()
+                loads[2].wait()
+
+            def body(group, carry):
+                for i in range(kept, chunks):
+                    terms[group, pl.ds((i - kept) * step, step), :] = out_term(i, group)
+                return carry
+
+            lax.fori_loop(0, line * cores, body, 0)
+        if 0 <= k - 1 < len(items):
+            fold(*items[k - 1])
+            flow(*items[k - 1], low)
+        if 0 <= k - 2 < len(items):
+            flow(*items[k - 2], jnp.logical_not(low))
+        if 0 <= k - 3 < len(items):
+            final(*items[k - 3])
+
+    for s in range(cycle):
+        here = (s == blk) & (owner == grp)
+
+        @pl.when(jnp.logical_not(here))
+        def _():
+            for r in range(per_half):
+                ref = g_out.at[s, pl.ds(r * step, step), :]
+                send(ref, ref, d_send.at[0, 0], d_recv.at[s, r], other, other).wait_recv()
+
+    for i in range(chunks):
+        for d in range(1, cycle):
+            t_copy(i, d).wait_send()
+        if i < per_half:
+            for s in range(cycle):
+                @pl.when(jnp.logical_not((s == blk) & (owner == grp)))
+                def _():
+                    s_copy(i, s).wait_send()
+        for j in range(share):
+            @pl.when(jnp.logical_not((grp * share + j == blk) & (grp == i // per_half)))
+            def _():
+                deliver(i, j).wait_send()
+
+    for kind, i in items:
+        cross(kind, i).wait_send()
+        for dest in range(line):
+            @pl.when(dest != pos)
+            def _():
+                hop(kind, i, 0, dest, other).wait_send()
+
+
+def combine(heads_t, heads_s, mix, t_out, s_out, cycle, cores, line, kept):
+    rows = heads_t.shape[1]
+    chunks = 2 * cores
+    step = rows // chunks
+    share = cycle // cores
+    groups = line * cores
+    wide = t_out.shape[1] // groups
+    t_width, s_width = t_out.shape[0], s_out.shape[0]
+    half = rows // cores
+    kind = jnp.bfloat16
+    any_space = pl.BlockSpec(memory_space=pl.ANY)
+    vmem = pl.BlockSpec(memory_space=pltpu.VMEM)
+    dma = pltpu.SemaphoreType.DMA
+    held = max(kept, 1)
+    rest = max(chunks - kept, 1)
+
+    def lines(n, width):
+        block = (n, line, step, width)
+        return [pltpu.VMEM(block, kind)] * 3 + [pltpu.VMEM((2,) + block, kind)]
+
+    def line_sems(n):
+        return [dma((n,)), dma((n,)), dma((n, line)), dma((2, n, line))]
+
+    return pl.pallas_call(
+        functools.partial(combine_kernel, cycle, cores, line, chunks, kept),
+        in_specs=[any_space] * 5,
+        out_specs=[vmem] * 3,
+        out_shape=[
+            jax.ShapeDtypeStruct((cycle, half, HD), kind),
+            jax.ShapeDtypeStruct((held * step, wide), jnp.float32),
+            jax.ShapeDtypeStruct((groups, rest * step, wide), kind),
+        ],
+        scratch_shapes=[
+            pltpu.VMEM(mix.shape, kind),
+            pltpu.VMEM(t_out.shape, kind),
+            pltpu.VMEM(s_out.shape, kind),
+            pltpu.VMEM((rows, t_width), kind),
+            pltpu.VMEM((rows, s_width), kind),
+        ]
+        + lines(chunks, s_width)
+        + lines(held, wide)
+        + [
+            pltpu.VMEM((step, wide), jnp.float32),
+            pltpu.VMEM((chunks, share, step, HD), kind),
+            dma((3,)),
+            dma((chunks, cycle - 1)),
+            dma((chunks, cycle - 1)),
+            dma((chunks,)),
+            dma((chunks // cores, cycle)),
+            dma((share, chunks)),
+            dma((chunks // cores,)),
+        ]
+        + line_sems(chunks)
+        + line_sems(held)
+        + [dma((chunks, share)), dma((cycle, chunks // cores))],
+        compiler_params=pltpu.CompilerParams(
+            collective_id=2, has_side_effects=True, vmem_limit_bytes=VMEM_LIMIT
+        ),
+        cost_estimate=pl.CostEstimate(
+            flops=0, bytes_accessed=64 * rows * wide * groups, transcendentals=0
+        ),
+    )(heads_t, heads_s, mix, t_out, s_out)
+
+
 def heads_on_chips(
     t_query, t_key, t_value, t_out, s_query, s_key, s_value, s_out, segments, selection
 ):
@@ -773,26 +1115,20 @@
 
     blended = pair_forward(per_blk, tables, pq, pk, pv)
     tables, blended, tq = lax.optimization_barrier((tables, blended, tq))
-    blended = lax.all_to_all(blended.reshape(cycle, half, HD), "blk", 0, 0, tiled=True)
-    blended = lax.all_to_all(blended, "grp", split_axis=0, concat_axis=1, tiled=True)
-    s_attn = blended.transpose(1, 0, 2).reshape(rows, share * HD)
 
     mix = jnp.concatenate([dot(s_rows, t_out, NT), dot(s_rows, s_out, NT)], axis=1)
     mix = lax.all_gather(mix.astype(jnp.bfloat16), "blk")
 
     whole = [x.reshape(cycle * rows, HD) for x in (tq, tk, tv)]
     whole_heads = teacher(*whole, 1, (1, (0, 0, 0)), jnp.int32(0), first_count)
-    t_attn = lax.all_to_all(whole_heads, "blk", split_axis=0, concat_axis=1, tiled=True)
-
-    grad_terms = project_grads(s_attn, t_attn, mix, groups)
-    grads = lax.psum_scatter(grad_terms, split, scatter_dimension=0, tiled=False)
-    terms = project(s_attn, t_attn, s_out, t_out, groups)
-    terms, grads = lax.optimization_barrier((terms, grads))
-    mismatch = lax.psum_scatter(terms, split, scatter_dimension=0, tiled=False)
-
-    grads = grads.reshape(rows, share, HD).transpose(1, 0, 2)
-    grads = lax.all_to_all(grads, "grp", split_axis=1, concat_axis=0, tiled=True)
-    grads = lax.all_to_all(grads, "blk", 0, 0, tiled=True).reshape(cycle * half, HD)
+
+    kept = 2
+    grads, near, terms = combine(
+        whole_heads.reshape(cycle, rows, HD), blended.reshape(cycle, half, HD), mix,
+        t_out, s_out, cycle, cores, groups // cores, kept,
+    )
+    rest = lax.psum_scatter(terms, split, scatter_dimension=0, tiled=False)
+    grads = grads.reshape(cycle * half, HD)
     dq, own, far = pair_backward(per_blk, cores, tables, pq, grads, pk, pv)
     out = depart(
         dq.reshape(cycle, half, HD),
@@ -801,7 +1137,8 @@
         cycle,
         cores,
     ).astype(jnp.float32)
-    return (mismatch.astype(jnp.float32), out[0], out[1], out[2])
+    mismatch = jnp.concatenate([near, rest.astype(jnp.float32)])
+    return (mismatch, out[0], out[1], out[2])
 
 
 def on_device(t_query, t_key, t_value, t_out, s_query, s_key, s_value, s_out, segments, selection):

time: 316 us -> 295 us (0.934)
  Pallas kernels: 177 us -> 259 us
  waiting for transfers between devices: 70.1 us -> 0.07 us
  blocking collectives: 20.7 us -> 0 us
  starting transfers between devices: 7.87 us -> 0.12 us
  local copies, waits for them, and re-layouts: 8.64 us -> 4.93 us
    pallas_call x2 -> x1, Pallas kernels: 21.4 us -> 97.2 us  [combine(): pl.pallas_call(functools.partial(combine_kernel, cycle, cores, line, chun...]
    reduce_scatter x2 -> x1, waiting for transfers between devices: 57.5 us -> 0.01 us  [heads_on_chips(): rest = lax.psum_scatter(terms, split, scatter_dimension=0, tiled=False)]
    all_to_all x3 -> x0, blocking collectives: 20.7 us -> none  [the longest x1 12.4 us: heads_on_chips(): lax.all_to_all(grads, 'blk', 0, 0, tiled=True).reshape(cycle * half, HD)]
    all_to_all x2 -> x0, waiting for transfers between devices: 12.5 us -> none  [the longest x1 12.5 us: heads_on_chips(): lax.all_to_all(whole_heads, 'blk', split_axis=0, concat_axis=1, tiled=True)]
    all_to_all x2 -> x0, starting transfers between devices: 7.75 us -> none  [the longest x1 4.12 us: heads_on_chips(): lax.all_to_all(whole_heads, 'blk', split_axis=0, concat_axis=1, tiled=True)]
    pallas_call x1, Pallas kernels: 29.3 us -> 33.7 us  [teacher(): pl.pallas_call(functools.partial(teacher_kernel, tile), grid_spec=pltpu.P...]
  transfers between devices with their start and end apart: 6 -> 3, of which waited for: 3 -> 0; matrix products, arithmetic and copies ran while one was open for 4% -> 3% of each run, Pallas kernels for 53% -> 55%
where the time goes in v3:
time: 295 us; the launch traced here: 296 us
  Pallas kernels  259 us (88%)
  between operations  13.9 us (5%)
  other arithmetic  9.49 us (3%)
  matrix products  8.36 us (3%)
  local copies, waits for them, and re-layouts  4.93 us (2%)
    pallas_call x1, Pallas kernels, combine(): pl.pallas_call(functools.partial(combine_kernel, cycle, cores, line, chun...  97.2 us
    pallas_call x1, Pallas kernels, arrive(): pl.pallas_call(functools.partial(arrive_kernel, cycle, cores), in_specs=[...  58.9 us
    pallas_call x1, Pallas kernels, teacher(): pl.pallas_call(functools.partial(teacher_kernel, tile), grid_spec=pltpu.P...  33.7 us
    pallas_call x1, Pallas kernels, pair_backward(): pl.pallas_call(functools.partial(pair_backward_kernel, per_blk), grid_spe...  27.5 us
    pallas_call x1, Pallas kernels, depart(): pl.pallas_call(functools.partial(depart_kernel, cycle, cores), in_specs=[...  24 us
    pallas_call x1, Pallas kernels, pair_forward(): pl.pallas_call(functools.partial(pair_forward_kernel, per_blk), grid_spec...  18.1 us
    dot_general x2, matrix products, dot(): return lax.dot_general(a, b, dims, preferred_element_type=jnp.float32)  8.36 us
  transfers between devices with their start and end apart: 3, of which 0 were waited for; matrix products, arithmetic and copies ran while one was open for 3% of the time, Pallas kernels for 55%

profile of v3, /device:TPU:0, one launch (start us, length us, event | category | flops | bytes accessed | tf_op | source)
XLA Modules:
  0.0 296.2 jit_solution(956182042889759393)
XLA Ops:
  7.2 0.0 all-gather.3.cloned.1.call-start
  7.2 0.0 copy-start.1
  7.2 2.0 constant_dynamic-slice_fusion
  9.2 0.0 all-gather.3.cloned.1.call-update
  9.3 0.0 all-gather.5.cloned.1.call-start
  9.3 1.3 pad_add_fusion.ints
  10.6 58.9 %shard_map.129 = (bf16[4,1024,128]{2,1,0:T(8,128)(2,1)}, bf16[4,1024,128]{2,1,0:T(8,128)(2,1)}, bf16[4,1024,128]{2,1,0:T(8,128)(2,1)}, bf16[4,512,128]{2,1,0:T(8...) custom-call(bf16[1024,512]{1,0:T(8,128)(2,1)} %tq.1, ...), custom_call_target="tpu_custom_call" | custom-call | bytes 67108864 | tf_op jit(solution)/shard_map/pallas_call | solution.py:450
  69.5 0.0 all-gather.3.cloned.1.call-done
  69.5 0.0 copy-done.1
  69.6 0.0 copy-start
  69.6 3.6 %fusion.1 = bf16[1,512,256]{1,2,0:T(8,128)(2,1)S(1)} fusion(bf16[512,4096]{1,0:T(8,128)(2,1)} %all-gather.3.cloned.1.call-done, bf16[256,4096]{1,0:T(8,128)(2,1)S(1)} %copy-done.1), kind=kOutput, calls=%fused_computation.4 | convolution fusion | flops 1073872896 | bytes 6553600 | tf_op jit(solution)/shard_map/dot_general | solution.py:22
  73.2 0.0 copy-done
  73.2 4.7 %fusion = bf16[1,512,512]{1,2,0:T(8,128)(2,1)S(1)} fusion(bf16[512,4096]{1,0:T(8,128)(2,1)} %all-gather.3.cloned.1.call-done, bf16[512,4096]{1,0:T(8,128)(2,1)S(1)} %copy-done), kind=kOutput, calls=%fused_computation.2 | convolution fusion | flops 2147745792 | bytes 8912896 | tf_op jit(solution)/shard_map/dot_general | solution.py:22
  78.0 0.0 copy-start.3
  78.0 0.1 pad_maximum_fusion.1
  78.0 1.2 copy.16
  79.2 0.0 all-gather.5.cloned.1.call-update
  79.2 0.0 reduce-scatter.2.cloned.1.call-start
  79.3 0.0 copy-done.3
  79.3 0.6 convert_reduce_fusion
  79.9 1.2 pad_add_fusion.1.info_ref
  81.1 1.3 pad_add_fusion.2.info_ref
  82.4 0.6 fusion.5
  83.1 18.1 %shard_map.130 = bf16[2048,128]{1,0:T(8,128)(2,1)} custom-call(s32[32,16]{1,0:T(8,128)} %get-tuple-element.37.sel_ref, s32[32,16]{1,0:T(8,128)} %get-tuple-element.38.place_ref, s32[3]{0:T(128)} %pad_add_fusion.2.info_ref, bf16[2048,128]{1,0:T(8,128)(2,1)} %bitcast.48, bf16[4096,128]{1,0:T(8,128)(2,1)} %bitcast.41, bf16[4096,128]{1,0:T(8,128)(2,1)} %bitcast.43), custom_call_target="tpu_custom_call" | custom-call | flops 17179869184 | bytes 2097152 | tf_op jit(solution)/shard_map/pallas_call | solution.py:691
  101.2 33.7 %shard_map.131 = bf16[4096,128]{1,0:T(8,128)(2,1)} custom-call(s32[2]{0:T(128)} %pad_add_fusion.1.info_ref, bf16[4096,128]{1,0:T(8,128)(2,1)} %bitcast.45, bf16[4096,128]{1,0:T(8,128)(2,1)} %bitcast.46, bf16[4096,128]{1,0:T(8,128)(2,1)} %bitcast.47), custom_call_target="tpu_custom_call" | custom-call | flops 4294967296 | bytes 4194304 | tf_op jit(solution)/shard_map/pallas_call | solution.py:83
  134.9 0.0 all-gather.5.cloned.1.call-done.mix_hbm
  134.9 97.2 %shard_map.132 = (bf16[4,512,128]{2,1,0:T(8,128)(2,1)}, f32[512,512]{1,0:T(8,128)}, bf16[8,512,512]{2,1,0:T(8,128)(2,1)}) custom-call(bf16[4,1024,128]{2,1,0:T(8,128)(2,1)} %bitcast.37, bf16[4,512,128]{2,1,0:T(8,128)(2,1)} %bitcast.39, bf16[4,512,768]{2,1,0:T(8,128)(2,1)} %all-gather.5.cloned.1.call-done.mix_hbm, bf16[512,4096]{1,0:T(8,128)(2,1)} %t_hbm.1, ...), custom_call_target="tpu_custom_call" | custom-call | bytes 268435456 | tf_op jit(solution)/shard_map/pallas_call | solution.py:1038
  232.1 0.0 reduce-scatter.2.cloned.1.call-update
  232.1 27.5 %shard_map.133 = (bf16[2048,128]{1,0:T(8,128)(2,1)}, f32[2,2048,128]{2,1,0:T(8,128)}, bf16[2,2048,128]{2,1,0:T(8,128)(2,1)}) custom-call(s32[32,16]{1,0:T(8,128)} %get-tuple-element.37.sel_ref, s32[32,16]{1,0:T(8,128)} %get-tuple-element.38.place_ref, s32[3]{0:T(128)} %pad_add_fusion.2.info_ref, bf16[2048,128]{1,0:T(8,128)(2,1)} %bitcast.49, ...), custom_call_target="tpu_custom_call" | custom-call | flops 34359738368 | bytes 4194304 | tf_op jit(solution)/shard_map/pallas_call | solution.py:715
  259.5 24.0 %shard_map.134 = bf16[3,1024,256]{2,1,0:T(8,128)(2,1)} custom-call(bf16[4,512,128]{2,1,0:T(8,128)(2,1)} %bitcast.38, f32[2,4,512,128]{3,2,1,0:T(8,128)} %bitcast.35, bf16[2,4,512,128]{3,2,1,0:T(8,128)(2,1)} %bitcast.36), custom_call_target="tpu_custom_call" | custom-call | tf_op jit(solution)/shard_map/pallas_call | solution.py:549
  283.6 1.7 convert_element_type.23
  285.2 0.0 copy-start.2
  285.2 1.7 slice_bitcast_fusion
  287.0 0.0 reduce-scatter.2.cloned.1.call-done
  287.0 1.2 bitcast_convert_fusion
  288.1 0.0 copy-done.2
  288.2 1.5 pad_maximum_fusion
  (1 shorter events, 0.0 us)
Async XLA Ops:
  7.2 62.4 %all-gather.3.cloned.1.call-start = ((), (), s32[]{:S(2)}) async-start(), calls=%async_computation.1 | async-start | bytes 4718592 | tf_op jit(solution)/shard_map/all_gather | solution.py:1095
  7.2 62.3 %copy-start.1 = (bf16[256,4096]{1,0:T(8,128)(2,1)S(1)}, bf16[256,4096]{1,0:T(8,128)(2,1)}, u32[]{:S(2)}) copy-start(bf16[256,4096]{1,0:T(8,128)(2,1)} %s_hbm.1) | copy-start | bytes 6291460
  9.3 125.6 %all-gather.5.cloned.1.call-start = ((), (), s32[]{:S(2)}) async-start(), calls=%async_computation.2 | async-start | bytes 3932160 | tf_op jit(solution)/shard_map/all_gather | solution.py:1120
  69.6 3.6 %copy-start = (bf16[512,4096]{1,0:T(8,128)(2,1)S(1)}, bf16[512,4096]{1,0:T(8,128)(2,1)}, u32[]{:S(2)}) copy-start(bf16[512,4096]{1,0:T(8,128)(2,1)} %t_hbm.1) | copy-start | bytes 12582916
  78.0 1.3 copy-start.3
  79.2 207.8 %reduce-scatter.2.cloned.1.call-start = ((), (), s32[]{:S(2)}) async-start(), calls=%async_computation.3 | async-start | bytes 4718592 | tf_op jit(solution)/shard_map/reduce_scatter | solution.py:1130
  285.2 2.9 copy-start.2
Sparse Core Ops, SparseCore 0:
  10.1 49.5 all-gather.2
  79.3 45.1 all-gather.4
  232.2 50.7 reduce-scatter.1

commit v4 on v3

--- a/solution.py
+++ b/solution.py
@@ -74,12 +74,11 @@
     o_ref[...] = (acc / total).T.astype(jnp.bfloat16)
 
 
-def teacher(queries, keys, values, heads, columns, offset, first_count):
+def teacher(info, queries, keys, values, heads, columns):
     rows, tokens = queries.shape[0], keys.shape[0]
     width = heads * HD
     step, (q_at, k_at, v_at) = columns
     tile = 512
-    info = jnp.stack([offset, first_count]).astype(jnp.int32)
     return pl.pallas_call(
         functools.partial(teacher_kernel, tile),
         grid_spec=pltpu.PrefetchScalarGridSpec(
@@ -307,7 +306,7 @@
 MESH = pl.DeviceIdType.MESH
 
 
-def greet(blk, grp, cycle, cores):
+def greet(blk, grp, cycle, cores, pos=None, line=1):
     barrier = pltpu.get_barrier_semaphore()
     for d in range(cycle):
         for e in range(cores):
@@ -318,7 +317,17 @@
                     device_id={"blk": lax.rem(blk + d, cycle), "grp": lax.rem(grp + e, cores)},
                     device_id_type=MESH,
                 )
-    pl.semaphore_wait(barrier, cycle * cores - 1)
+    ends = 0
+    if pos is not None:
+        for ahead, there in ((-1, pos > 0), (1, pos < line - 1)):
+            @pl.when(there)
+            def _():
+                pl.semaphore_signal(
+                    barrier, inc=1, device_id={"head": pos + ahead}, device_id_type=MESH
+                )
+
+            ends = ends + jnp.where(there, 1, 0)
+    pl.semaphore_wait(barrier, cycle * cores - 1 + ends)
 
 
 def send(src, dst, send_sem, recv_sem, blk, grp):
@@ -333,34 +342,36 @@
 
 
 def arrive_kernel(
-    cycle, cores, tq, tk, tv, sq, sk, sv, ints,
-    oq, ok, ov, pq, pk, pv, oints,
-    t_stage, s_stage, local, s_send, s_recv, x_send, x_recv, t_send, t_recv, i_send, i_recv,
+    cycle, cores, line, picks, tq, tk, tv, sq, sk, sv, ints, t_hbm, s_hbm,
+    oq, ok, ov, pq, pk, pv, oints, info, mix, blended,
+    t_stage, s_stage, rows_all, t_w, s_w, table, q_wide, k_sel, v_sel,
+    local, w_sem, s_send, s_recv, x_send, x_recv, t_send, t_recv, i_send, i_recv,
+    z_send, z_recv, zx_send, zx_recv,
 ):
-    blk, grp = lax.axis_index("blk"), lax.axis_index("grp")
+    blk, grp, pos = lax.axis_index("blk"), lax.axis_index("grp"), lax.axis_index("head")
     rows = tq.shape[0]
     half = rows // cores
     share = cycle // cores
     owner = blk // share
-    greet(blk, grp, cycle, cores)
-
-    def student_copy(t, j, e):
-        src = (sq, sk, sv)[t].at[pl.ds(e * half, half), pl.ds(j * HD, HD)]
-        dst = (pq.at[blk], pk.at[e, blk], pv.at[e, blk])[t]
-        return src, dst
-
-    def student_send(t, j, e):
-        return send(
-            *student_copy(t, j, e), s_send.at[t, j, e], s_recv.at[t, blk], grp * share + j, e
+    other = lax.rem(grp + 1, cores)
+    depth = rows_all.shape[2]
+    teacher_sets = ((tk, ok), (tv, ov), (tq, oq))
+    own_columns = pl.ds(pl.multiple_of(blk * HD, HD), HD)
+    own_rows = s_hbm.at[pl.ds(pl.multiple_of(blk * depth, depth), depth), :]
+
+    loads = [
+        pltpu.make_async_copy(src, dst, w_sem.at[n])
+        for n, (src, dst) in enumerate(
+            ((own_rows, rows_all.at[pos, grp]), (t_hbm, t_w), (s_hbm, s_w))
         )
-
-    pieces = [(t, j, e) for t in (1, 2, 0) for j in range(share) for e in range(cores)]
-    for t, j, e in pieces:
-        mine = (grp * share + j == blk) & (grp == e)
-
-        @pl.when(jnp.logical_not(mine))
-        def _():
-            student_send(t, j, e).start()
+    ]
+    inward = [
+        pltpu.make_async_copy(src.at[:, own_columns], t_stage.at[t], local.at[t])
+        for t, (src, dst) in enumerate(teacher_sets)
+    ]
+    for load in loads + inward:
+        load.start()
+    greet(blk, grp, cycle, cores, pos, line)
 
     int_copies = [
         send(ints, oints.at[blk], i_send.at[d - 1], i_recv.at[d - 1], lax.rem(blk + d, cycle), grp)
@@ -370,8 +381,80 @@
         copy.start()
     oints[blk] = ints[...]
 
+    per_half = half // BS
+
+    def token_blocks(s, e):
+        return pl.ds((s * cores + e) * per_half, per_half)
+
+    def student_copy(t, j, e):
+        columns = pl.ds(j * HD, HD)
+        if t == 0:
+            return sq.at[pl.ds(e * half, half), columns], pq.at[blk]
+        src, dst = (sk, pk) if t == 1 else (sv, pv)
+        return src.at[pl.ds(e * per_half, per_half), :, columns], dst.at[token_blocks(blk, e)]
+
+    def student_send(t, j, e):
+        return send(
+            *student_copy(t, j, e), s_send.at[t, j, e], s_recv.at[t, blk], grp * share + j, e
+        )
+
+    pieces = [(t, j, e) for t in (1, 2, 0) for j in range(share) for e in range(cores)]
+
+    def is_mine(j, e):
+        return (grp * share + j == blk) & (grp == e)
+
+    for t, j, e in pieces:
+        @pl.when(jnp.logical_not(is_mine(j, e)))
+        def _():
+            student_send(t, j, e).start()
+
+    def relay(way, step, origin, src):
+        return pltpu.make_async_remote_copy(
+            src_ref=src,
+            dst_ref=rows_all.at[origin, grp],
+            send_sem=z_send.at[way, step],
+            recv_sem=z_recv.at[origin],
+            device_id={"head": pos + (1 if way == 0 else -1)},
+            device_id_type=MESH,
+        )
+
+    def share_rows(origin, src):
+        dst = rows_all.at[origin, grp]
+        return send(src, dst, zx_send.at[origin], zx_recv.at[origin], blk, other)
+
+    ahead = (pos < line - 1, pos > 0)
+
+    for way in (0, 1):
+        @pl.when(ahead[way])
+        def _():
+            relay(way, 0, pos, own_rows).start()
+
+    share_rows(pos, own_rows).start()
+
+    def relay_step(step):
+        for way in (0, 1):
+            origin = pos - step if way == 0 else pos + step
+            exists = origin >= 0 if way == 0 else origin < line
+
+            @pl.when(exists)
+            def _():
+                src = rows_all.at[origin, grp]
+                pltpu.make_async_remote_copy(
+                    src_ref=src,
+                    dst_ref=src,
+                    send_sem=z_send.at[way, step],
+                    recv_sem=z_recv.at[origin],
+                    device_id={"grp": other},
+                    device_id_type=MESH,
+                ).wait_recv()
+                share_rows(origin, src).start()
+
+                @pl.when(ahead[way])
+                def _():
+                    relay(way, step, origin, src).start()
+
     t_copies = []
-    for t, (src, dst) in enumerate(((tk, ok), (tv, ov), (tq, oq))):
+    for t, (src, dst) in enumerate(teacher_sets):
         for d in range(1, cycle):
             dest = lax.rem(blk + d, cycle)
             columns = pl.ds(pl.multiple_of(dest * HD, HD), HD)
@@ -383,81 +466,158 @@
     for copy in t_copies:
         copy.start()
 
-    columns = pl.ds(pl.multiple_of(blk * HD, HD), HD)
-    for t, (src, dst) in enumerate(((tk, ok), (tv, ov), (tq, oq))):
-        pltpu.make_async_copy(src.at[:, columns], t_stage.at[t], local.at[t]).start()
-    for t, (src, dst) in enumerate(((tk, ok), (tv, ov), (tq, oq))):
-        pltpu.make_async_copy(src.at[:, columns], t_stage.at[t], local.at[t]).wait()
-        pltpu.make_async_copy(t_stage.at[t], dst.at[blk], local.at[t]).start()
-    for t, (src, dst) in enumerate(((tk, ok), (tv, ov), (tq, oq))):
-        pltpu.make_async_copy(t_stage.at[t], dst.at[blk], local.at[t]).wait()
+    outward = [
+        pltpu.make_async_copy(t_stage.at[t], dst.at[blk], local.at[t])
+        for t, (src, dst) in enumerate(teacher_sets)
+    ]
+    for t in range(3):
+        inward[t].wait()
+        outward[t].start()
+    for t in range(3):
+        outward[t].wait()
 
     for t, j, e in pieces:
-        mine = (grp * share + j == blk) & (grp == e)
-
-        @pl.when(mine)
+        @pl.when(is_mine(j, e))
         def _():
             src, dst = student_copy(t, j, e)
-            inward = pltpu.make_async_copy(src, s_stage, local.at[0])
-            inward.start()
-            inward.wait()
-            outward = pltpu.make_async_copy(s_stage, dst, local.at[0])
-            outward.start()
-            outward.wait()
-
-    other = lax.rem(grp + 1, cores)
-
-    def arrival(t, s):
-        dst = (pq.at[s], pk.at[grp, s], pv.at[grp, s])[t]
-        return send(dst, dst, s_send.at[t, 0, 0], s_recv.at[t, s], other, other)
+            copy = pltpu.make_async_copy(src, dst, local.at[t])
+            copy.start()
+            copy.wait()
+
+    def piece_of(t, s):
+        return (pq.at[s], pk.at[token_blocks(s, grp)], pv.at[token_blocks(s, grp)])[t]
 
     def cross(t, s):
-        ref = (None, pk, pv)[t].at[grp, s]
+        ref = piece_of(t, s)
         return send(ref, ref, x_send.at[t - 1, s], x_recv.at[t - 1, s], blk, other)
 
     for t in (1, 2, 0):
         for s in range(cycle):
-            remote = jnp.logical_not((s == blk) & (owner == grp))
-
-            @pl.when(remote)
-            def _():
-                arrival(t, s).wait_recv()
+            @pl.when(jnp.logical_not((s == blk) & (owner == grp)))
+            def _():
+                ref = piece_of(t, s)
+                send(ref, ref, s_send.at[t, 0, 0], s_recv.at[t, s], other, other).wait_recv()
 
             if t:
                 cross(t, s).start()
-
+        if t == 1:
+            relay_step(1)
+    for copy in int_copies:
+        copy.wait()
+    to_table = pltpu.make_async_copy(oints, table, local.at[0])
+    to_table.start()
+    seg_rows = ints.shape[0] - rows // BS
+    first_count = jnp.sum((oints[:, :seg_rows, :] == 0).astype(jnp.float32)).astype(jnp.int32)
+    info[0] = 0
+    info[1] = first_count
+    info[2] = grp
+    info[3] = 0
+    q_wide[...] = jnp.zeros_like(q_wide)
     for t in (1, 2):
         for s in range(cycle):
             cross(t, s).wait()
-    for copy in int_copies + t_copies:
+    to_table.wait()
+
+    mine = half // BS
+    pairs = cycle * half // (2 * BS)
+
+    def pair_step(pair, carry):
+        @pl.when(pair == pairs // 8)
+        def _():
+            relay_step(2)
+
+        source, inside = pair * 2 // mine, lax.rem(pair * 2, mine)
+        first_row = pl.multiple_of(inside * BS, 2 * BS)
+        spread_pair(pq.at[source, pl.ds(first_row, 2 * BS), :], q_wide)
+        at = grp * mine + inside
+
+        def chosen(h, e):
+            return table[source, seg_rows + at + h, e]
+
+        weights, total = pair_weights(
+            chosen, picks, source * (rows // BS) + at, first_count, q_wide, pk, pv, k_sel, v_sel
+        )
+        weights = (weights / total).astype(jnp.bfloat16)
+        value = dot(weights, v_sel[...], TN)
+        for h in range(2):
+            blended[source, pl.ds(first_row + h * BS, BS), :] = value[
+                h * BS : (h + 1) * BS, h * HD : (h + 1) * HD
+            ].astype(jnp.bfloat16)
+        return carry
+
+    lax.fori_loop(0, pairs, pair_step, 0)
+    relay_step(3)
+
+    for load in loads:
+        load.wait()
+    for origin in range(line):
+        share_rows(origin, rows_all.at[origin, grp]).wait_recv()
+    gathered = rows_all.shape[0] * rows_all.shape[1] * depth
+    width = 2 * HD
+    for w, base in ((t_w, 0), (s_w, t_w.shape[0])):
+        def gram(n, carry):
+            at = pl.multiple_of(n * width, width)
+            value = dot(rows_all[...].reshape(gathered, w.shape[1]), w[pl.ds(at, width), :], NT)
+            mix[:, pl.ds(pl.multiple_of(base + at, width), width)] = value.astype(jnp.bfloat16)
+            return carry
+
+        lax.fori_loop(0, w.shape[0] // width, gram, 0)
+
+    for copy in t_copies:
         copy.wait()
     for t, j, e in pieces:
-        mine = (grp * share + j == blk) & (grp == e)
-
-        @pl.when(jnp.logical_not(mine))
+        @pl.when(jnp.logical_not(is_mine(j, e)))
         def _():
             student_send(t, j, e).wait_send()
-
-
-def arrive(t_query, t_key, t_value, s_query, s_key, s_value, ints, cycle, cores):
+    for origin in range(line):
+        share_rows(origin, rows_all.at[origin, grp]).wait_send()
+    for way in (0, 1):
+        for step in range(line - 1):
+            origin = pos - step if way == 0 else pos + step
+            exists = origin >= 0 if way == 0 else origin < line
+
+            @pl.when(exists & ahead[way])
+            def _():
+                relay(way, step, origin, rows_all.at[origin, grp]).wait_send()
+
+
+def arrive(t_query, t_key, t_value, t_out, s_query, s_key, s_value, s_out, ints, picks, sizes):
+    cycle, cores, line = sizes
     rows = t_query.shape[0]
     half = rows // cores
     share = cycle // cores
+    depth = s_out.shape[0] // cycle
     kind = t_query.dtype
     any_space = pl.BlockSpec(memory_space=pl.ANY)
     vmem = pl.BlockSpec(memory_space=pltpu.VMEM)
     dma = pltpu.SemaphoreType.DMA
     return pl.pallas_call(
-        functools.partial(arrive_kernel, cycle, cores),
-        in_specs=[any_space] * 6 + [vmem],
-        out_specs=[any_space] * 6 + [vmem],
+        functools.partial(arrive_kernel, cycle, cores, line, picks),
+        in_specs=[any_space] * 6 + [vmem] + [any_space] * 2,
+        out_specs=[any_space] * 3
+        + [vmem] * 4
+        + [pl.BlockSpec(memory_space=pltpu.SMEM)]
+        + [vmem] * 2,
         out_shape=[jax.ShapeDtypeStruct((cycle, rows, HD), kind)] * 3
         + [jax.ShapeDtypeStruct((cycle, half, HD), kind)]
-        + [jax.ShapeDtypeStruct((cores, cycle, half, HD), kind)] * 2
-        + [jax.ShapeDtypeStruct((cycle,) + ints.shape, ints.dtype)],
+        + [jax.ShapeDtypeStruct((cycle * rows // BS, BS, HD), kind)] * 2
+        + [
+            jax.ShapeDtypeStruct((cycle,) + ints.shape, ints.dtype),
+            jax.ShapeDtypeStruct((4,), jnp.int32),
+            jax.ShapeDtypeStruct((line * cores * depth, t_out.shape[0] + s_out.shape[0]), kind),
+            jax.ShapeDtypeStruct((cycle, half, HD), kind),
+        ],
         scratch_shapes=[
             pltpu.VMEM((3, rows, HD), kind),
             pltpu.VMEM((half, HD), kind),
+            pltpu.VMEM((line, cores, depth, s_out.shape[1]), kind),
+            pltpu.VMEM(t_out.shape, kind),
+            pltpu.VMEM(s_out.shape, kind),
+            pltpu.SMEM((cycle,) + ints.shape, ints.dtype),
+        ]
+        + pair_scratch(picks * BS, 1)
+        + [
+            dma((3,)),
             dma((3,)),
             dma((3, share, cores)),
             dma((3, cycle)),
@@ -467,27 +627,33 @@
             dma((3, cycle - 1)),
             dma((cycle - 1,)),
             dma((cycle - 1,)),
+            dma((2, line)),
+            dma((line,)),
+            dma((line,)),
+            dma((line,)),
         ],
         compiler_params=pltpu.CompilerParams(
             collective_id=0, has_side_effects=True, vmem_limit_bytes=VMEM_LIMIT
         ),
-        cost_estimate=pl.CostEstimate(
-            flops=0, bytes_accessed=64 * rows * HD * 2 * cycle, transcendentals=0
-        ),
-    )(t_query, t_key, t_value, s_query, s_key, s_value, ints)
-
-
-def depart_kernel(cycle, cores, dq, own, far, out, got, mine, x_send, x_recv, d_send, d_recv):
-    blk, grp = lax.axis_index("blk"), lax.axis_index("grp")
+    )(t_query, t_key, t_value, s_query, s_key, s_value, ints, t_out, s_out)
+
+
+def depart_kernel(
+    cycle, cores, line, parts, dq, own, far, terms, out_q, out_k, out_v, m_out,
+    got, mine, m_own, m_got, m_line, total,
+    x_send, x_recv, d_send, d_recv, mx_send, mx_recv, mz_send, mz_recv,
+):
+    blk, grp, pos = lax.axis_index("blk"), lax.axis_index("grp"), lax.axis_index("head")
     half = dq.shape[1]
     share = cycle // cores
     owner, slot = blk // share, lax.rem(blk, share)
     other = lax.rem(grp + 1, cores)
-    greet(blk, grp, cycle, cores)
+    step = m_own.shape[2]
+    greet(blk, grp, cycle, cores, pos, line)
 
     def target(t, j, e):
         rows = pl.ds(pl.multiple_of(e * half, half), half)
-        return out.at[t, rows, pl.ds(pl.multiple_of(j * HD, HD), HD)]
+        return (out_q, out_k, out_v)[t].at[rows, pl.ds(pl.multiple_of(j * HD, HD), HD)]
 
     def source(t, s):
         return dq.at[s] if t == 0 else mine.at[t - 1, s]
@@ -509,19 +675,94 @@
         def _():
             target(t, slot, grp)[...] = source(t, s)[...]
 
+    def term_cross(n, z):
+        return send(
+            terms.at[z * cores + other, pl.ds(n * step, step), :],
+            m_got.at[n, z],
+            mx_send.at[n, z],
+            mx_recv.at[n, z],
+            blk,
+            other,
+        )
+
+    def hop(n, way, dest, there):
+        return pltpu.make_async_remote_copy(
+            src_ref=m_own.at[n, dest],
+            dst_ref=m_line.at[way, n, dest],
+            send_sem=mz_send.at[n, dest],
+            recv_sem=mz_recv.at[way, n, dest],
+            device_id={"head": there},
+            device_id_type=MESH,
+        )
+
+    def fold(n):
+        for z in range(line):
+            term_cross(n, z).wait_recv()
+            m_own[n, z] = (
+                terms[z * cores + grp, pl.ds(n * step, step), :].astype(jnp.float32)
+                + m_got[n, z].astype(jnp.float32)
+            ).astype(jnp.bfloat16)
+
+    def flow(n, upward):
+        way = jnp.where(upward, 0, 1)
+        there = jnp.where(upward, pos + 1, pos - 1)
+        count = jnp.where(upward, line - 1 - pos, pos)
+        fed = jnp.where(upward, pos, line - 1 - pos) > 0
+
+        def body(k, carry):
+            dest = jnp.where(upward, line - 1 - k, k)
+
+            @pl.when(fed)
+            def _():
+                hop(n, way, dest, there).wait_recv()
+                m_own[n, dest] = (
+                    m_own[n, dest].astype(jnp.float32) + m_line[way, n, dest].astype(jnp.float32)
+                ).astype(jnp.bfloat16)
+
+            hop(n, way, dest, there).start()
+            return carry
+
+        lax.fori_loop(0, count, body, 0)
+
+    def final(n):
+        total[...] = m_own[n, pos].astype(jnp.float32)
+        for way, fed in ((0, pos > 0), (1, pos < line - 1)):
+            @pl.when(fed)
+            def _():
+                hop(n, way, pos, pos).wait_recv()
+                total[...] += m_line[way, n, pos].astype(jnp.float32)
+
+        m_out[n * step : (n + 1) * step, :] = total[...]
+
     crossing = [
         send(far.at[t], got.at[t], x_send.at[t], x_recv.at[t], blk, other) for t in range(2)
     ]
+    for z in range(line):
+        term_cross(0, z).start()
     for copy in crossing:
         copy.start()
+    for n in range(1, parts):
+        for z in range(line):
+            term_cross(n, z).start()
     for s in range(cycle):
         emit(0, s)
+    low = pos < line // 2
+    fold(0)
+    flow(0, low)
     for t in range(2):
         crossing[t].wait_recv()
         for s in range(cycle):
             mine[t, s] = (own[t, s] + got[t, s].astype(jnp.float32)).astype(jnp.bfloat16)
         for s in range(cycle):
             emit(t + 1, s)
+    for n in range(parts + 1):
+        if 0 < n < parts:
+            fold(n)
+            flow(n, low)
+        if n:
+            flow(n - 1, jnp.logical_not(low))
+    for n in range(parts):
+        final(n)
     for copy in crossing:
         copy.wait_send()
     for t in range(3):
@@ -540,57 +781,71 @@
             def _():
                 piece(t, s).wait_send()
 
-
-def depart(dq, own, far, cycle, cores):
+    for n in range(parts):
+        for dest in range(line):
+            term_cross(n, dest).wait_send()
+
+            @pl.when(dest != pos)
+            def _():
+                hop(n, 0, dest, other).wait_send()
+
+
+def depart(dq, own, far, terms, cycle, cores, line):
     half = dq.shape[1]
     share = cycle // cores
+    parts = 2
+    rows, wide = terms.shape[1:]
+    step = rows // parts
+    kind = jnp.bfloat16
     vmem = pl.BlockSpec(memory_space=pltpu.VMEM)
     dma = pltpu.SemaphoreType.DMA
+    block = (parts, line, step, wide)
     return pl.pallas_call(
-        functools.partial(depart_kernel, cycle, cores),
-        in_specs=[vmem] * 3,
-        out_specs=vmem,
-        out_shape=jax.ShapeDtypeStruct((3, cores * half, share * HD), jnp.bfloat16),
+        functools.partial(depart_kernel, cycle, cores, line, parts),
+        in_specs=[vmem] * 4,
+        out_specs=[vmem] * 4,
+        out_shape=[jax.ShapeDtypeStruct((cores * half, share * HD), kind)] * 3
+        + [jax.ShapeDtypeStruct((rows, wide), jnp.float32)],
         scratch_shapes=[
-            pltpu.VMEM((2, cycle, half, HD), jnp.bfloat16),
-            pltpu.VMEM((2, cycle, half, HD), jnp.bfloat16),
+            pltpu.VMEM((2, cycle, half, HD), kind),
+            pltpu.VMEM((2, cycle, half, HD), kind),
+            pltpu.VMEM(block, kind),
+            pltpu.VMEM(block, kind),
+            pltpu.VMEM((2,) + block, kind),
+            pltpu.VMEM((step, wide), jnp.float32),
             dma((2,)),
             dma((2,)),
             dma((3, cycle)),
             dma((3, share, cores)),
+            dma((parts, line)),
+            dma((parts, line)),
+            dma((parts, line)),
+            dma((2, parts, line)),
         ],
         compiler_params=pltpu.CompilerParams(
             collective_id=1, has_side_effects=True, vmem_limit_bytes=VMEM_LIMIT
         ),
-    )(dq, own, far)
-
-
-def pair_weights(sel_ref, place_ref, info_ref, per_blk, q_wide, k_all, v_all, k_sel, v_sel):
-    pair = pl.program_id(0)
-    count = sel_ref.shape[1]
-    first_count, grp = info_ref[0], info_ref[1]
-    mine = per_blk // info_ref[2]
-
-    def query_block(index):
-        return (index // mine) * per_blk + grp * mine + lax.rem(index, mine)
-
+    )(dq, own, far, terms)
+
+
+def pair_weights(
+    chosen, count, query_block, first_count, q_wide, k_all, v_all, k_sel, v_sel
+):
     for e in range(count):
         for h in range(2):
-            source = pl.ds(pl.multiple_of(place_ref[2 * pair + h, e] * BS, BS), BS)
+            source = chosen(h, e)
             cols = slice(h * HD, (h + 1) * HD)
-            k_sel[e * BS : (e + 1) * BS, cols] = k_all[source, :]
-            v_sel[e * BS : (e + 1) * BS, cols] = v_all[source, :]
+            k_sel[e * BS : (e + 1) * BS, cols] = k_all[source]
+            v_sel[e * BS : (e + 1) * BS, cols] = v_all[source]
     within = lax.broadcasted_iota(jnp.int32, (BS, 1), 0)
     lane = lax.broadcasted_iota(jnp.int32, (1, 2 * BS), 1)
     second = lane >= BS
-    query_pos = (
-        jnp.where(second, query_block(2 * pair + 1), query_block(2 * pair)) * BS + lax.rem(lane, BS)
-    )
+    query_pos = query_block * BS + lane
     low = jnp.where(query_pos < first_count, 0, first_count)
     scores = dot(k_sel[...], q_wide[...], NT)
     allowed = []
     for e in range(count):
-        base = jnp.where(second, sel_ref[2 * pair + 1, e], sel_ref[2 * pair, e]) * BS
+        base = jnp.where(second, chosen(1, e), chosen(0, e)) * BS
         allowed.append((within <= query_pos - base) & (within >= low - base))
     scores = jnp.concatenate(
         [jnp.where(a, scores[e * BS : (e + 1) * BS], MASKED) for e, a in enumerate(allowed)]
@@ -610,27 +865,8 @@
         )
 
 
-def pair_forward_kernel(
-    per_blk, sel_ref, place_ref, info_ref, q_ref, k_all, v_all, o_ref, q_wide, k_sel, v_sel
-):
-    @pl.when(pl.program_id(0) == 0)
-    def _():
-        q_wide[...] = jnp.zeros_like(q_wide)
-
-    spread_pair(q_ref, q_wide)
-    weights, total = pair_weights(
-        sel_ref, place_ref, info_ref, per_blk, q_wide, k_all, v_all, k_sel, v_sel
-    )
-    weights = (weights / total).astype(jnp.bfloat16)
-    blended = dot(weights, v_sel[...], TN)
-    for h in range(2):
-        o_ref[h * BS : (h + 1) * BS, :] = blended[
-            h * BS : (h + 1) * BS, h * HD : (h + 1) * HD
-        ].astype(jnp.bfloat16)
-
-
 def pair_backward_kernel(
-    per_blk, sel_ref, place_ref, info_ref, q_ref, g_ref, k_all, v_all, dq_ref, own_ref, far_ref,
+    picks, rows, table, info_ref, q_ref, g_ref, k_all, v_all, dq_ref, own_ref, far_ref,
     dk_sum, dv_sum, q_wide, g_wide, k_sel, v_sel,
 ):
     pair = pl.program_id(0)
@@ -644,8 +880,17 @@
 
     spread_pair(q_ref, q_wide)
     spread_pair(g_ref, g_wide)
+    cycle, half = own_ref.shape[1], own_ref.shape[2]
+    mine = half // BS
+    source, inside = pair * 2 // mine, lax.rem(pair * 2, mine)
+    at = info_ref[2] * mine + inside
+    seg_rows = table.shape[1] - rows // BS
+
+    def chosen(h, e):
+        return table[source, seg_rows + at + h, e]
+
     weights, total = pair_weights(
-        sel_ref, place_ref, info_ref, per_blk, q_wide, k_all, v_all, k_sel, v_sel
+        chosen, picks, source * (rows // BS) + at, info_ref[1], q_wide, k_all, v_all, k_sel, v_sel
     )
     weights = weights / total
     weight_grad = dot(v_sel[...], g_wide[...], NT)
@@ -658,22 +903,21 @@
         ].astype(jnp.bfloat16)
     key_grad = dot(score_grad, q_wide[...])
     value_grad = dot(weights.astype(jnp.bfloat16), g_wide[...])
-    for e in range(sel_ref.shape[1]):
+    for e in range(picks):
         for h in range(2):
-            target = pl.ds(pl.multiple_of(place_ref[2 * pair + h, e] * BS, BS), BS)
+            target = pl.ds(pl.multiple_of(chosen(h, e) * BS, BS), BS)
             cols = slice(h * HD, (h + 1) * HD)
             dk_sum[target, :] += key_grad[e * BS : (e + 1) * BS, cols]
             dv_sum[target, :] += value_grad[e * BS : (e + 1) * BS, cols]
 
     @pl.when(pair == pl.num_programs(0) - 1)
     def _():
-        part = own_ref.shape[1]
-        near = pl.ds(pl.multiple_of(info_ref[1] * part, part), part)
-        away = pl.ds(pl.multiple_of((info_ref[2] - 1 - info_ref[1]) * part, part), part)
-        own_ref[0] = dk_sum[near, :]
-        own_ref[1] = dv_sum[near, :]
-        far_ref[0] = dk_sum[away, :].astype(jnp.bfloat16)
-        far_ref[1] = dv_sum[away, :].astype(jnp.bfloat16)
+        for s in range(cycle):
+            near = pl.ds(pl.multiple_of(s * rows + info_ref[2] * half, half), half)
+            away = pl.ds(pl.multiple_of((s + 1) * rows - (info_ref[2] + 1) * half, half), half)
+            for t, total in enumerate((dk_sum, dv_sum)):
+                own_ref[t, s] = total[near, :]
+                far_ref[t, s] = total[away, :].astype(jnp.bfloat16)
 
 
 def pair_scratch(keys, wides):
@@ -683,55 +927,35 @@
     ]
 
 
-def pair_forward(per_blk, tables, queries, keys, values):
-    rows, width = queries.shape
-    tokens = keys.shape[0]
-    row_block = pl.BlockSpec((2 * BS, width), lambda b, *_: (b, 0))
-    whole = pl.BlockSpec((tokens, width), lambda b, *_: (0, 0))
+def pair_backward(table, info, picks, queries, grads, keys, values):
+    cycle, half, width = queries.shape
+    tokens = keys.shape[0] * BS
+    per_step = half // (2 * BS)
+    row_block = pl.BlockSpec((None, 2 * BS, width), lambda b, *_: (b // per_step, b % per_step, 0))
+    whole = pl.BlockSpec(keys.shape, lambda b, *_: (0, 0, 0))
+    both = pl.BlockSpec((2, cycle, half, width), lambda b, *_: (0, 0, 0, 0))
     return pl.pallas_call(
-        functools.partial(pair_forward_kernel, per_blk),
+        functools.partial(pair_backward_kernel, picks, tokens // cycle),
         grid_spec=pltpu.PrefetchScalarGridSpec(
-            num_scalar_prefetch=3,
-            grid=(rows // (2 * BS),),
-            in_specs=[row_block, whole, whole],
-            out_specs=row_block,
-            scratch_shapes=pair_scratch(tables[0].shape[1] * BS, 1),
-        ),
-        out_shape=jax.ShapeDtypeStruct((rows, width), jnp.bfloat16),
-        compiler_params=pltpu.CompilerParams(vmem_limit_bytes=VMEM_LIMIT),
-        cost_estimate=pl.CostEstimate(
-            flops=16 * rows * tokens * width, bytes_accessed=4 * tokens * width, transcendentals=0
-        ),
-    )(*tables, queries, keys, values)
-
-
-def pair_backward(per_blk, cores, tables, queries, grads, keys, values):
-    rows, width = queries.shape
-    tokens = keys.shape[0]
-    part = tokens // cores
-    row_block = pl.BlockSpec((2 * BS, width), lambda b, *_: (b, 0))
-    whole = pl.BlockSpec((tokens, width), lambda b, *_: (0, 0))
-    both = pl.BlockSpec((2, part, width), lambda b, *_: (0, 0, 0))
-    return pl.pallas_call(
-        functools.partial(pair_backward_kernel, per_blk),
-        grid_spec=pltpu.PrefetchScalarGridSpec(
-            num_scalar_prefetch=3,
-            grid=(rows // (2 * BS),),
+            num_scalar_prefetch=2,
+            grid=(cycle * per_step,),
             in_specs=[row_block, row_block, whole, whole],
             out_specs=[row_block, both, both],
             scratch_shapes=[pltpu.VMEM((tokens, width), jnp.float32)] * 2
-            + pair_scratch(tables[0].shape[1] * BS, 2),
+            + pair_scratch(picks * BS, 2),
         ),
         out_shape=[
-            jax.ShapeDtypeStruct((rows, width), jnp.bfloat16),
-            jax.ShapeDtypeStruct((2, part, width), jnp.float32),
-            jax.ShapeDtypeStruct((2, part, width), jnp.bfloat16),
+            jax.ShapeDtypeStruct((cycle, half, width), jnp.bfloat16),
+            jax.ShapeDtypeStruct((2, cycle, half, width), jnp.float32),
+            jax.ShapeDtypeStruct((2, cycle, half, width), jnp.bfloat16),
         ],
         compiler_params=pltpu.CompilerParams(vmem_limit_bytes=VMEM_LIMIT),
         cost_estimate=pl.CostEstimate(
-            flops=32 * rows * tokens * width, bytes_accessed=8 * tokens * width, transcendentals=0
+            flops=32 * cycle * half * tokens * width,
+            bytes_accessed=8 * tokens * width,
+            transcendentals=0,
         ),
-    )(*tables, queries, grads, keys, values)
+    )(table, info, queries, grads, keys, values)
 
 
 def combine_kernel(
@@ -740,6 +964,7 @@
     mix, t_w, s_w, t_attn, s_attn, g_own, g_far, g_got, g_line, m_own, m_far, m_got, m_line,
     total, g_done, w_sem, t_send, t_recv, t_local, s_send, s_recv, s_local,
     gx_send, gx_recv, gz_send, gz_recv, mx_send, mx_recv, mz_send, mz_recv, d_send, d_recv,
+    p_send, p_recv,
 ):
     blk, grp, pos = lax.axis_index("blk"), lax.axis_index("grp"), lax.axis_index("head")
     share = cycle // cores
@@ -750,30 +975,12 @@
 
     loads = [
         pltpu.make_async_copy(src, dst, w_sem.at[n])
-        for n, (src, dst) in enumerate(((mix_hbm, mix), (t_hbm, t_w), (s_hbm, s_w)))
+        for n, (src, dst) in enumerate(((mix_hbm, mix.at[blk]), (t_hbm, t_w), (s_hbm, s_w)))
     ]
     for load in loads:
         load.start()
 
-    barrier = pltpu.get_barrier_semaphore()
-    for d in range(cycle):
-        for e in range(cores):
-            if d or e:
-                pl.semaphore_signal(
-                    barrier,
-                    inc=1,
-                    device_id={"blk": lax.rem(blk + d, cycle), "grp": lax.rem(grp + e, cores)},
-                    device_id_type=MESH,
-                )
-    for ahead, there in ((-1, pos > 0), (1, pos < line - 1)):
-        @pl.when(there)
-        def _():
-            pl.semaphore_signal(
-                barrier, inc=1, device_id={"head": pos + ahead}, device_id_type=MESH
-            )
-
-    ends = jnp.where(pos > 0, 1, 0) + jnp.where(pos < line - 1, 1, 0)
-    pl.semaphore_wait(barrier, cycle * cores - 1 + ends)
+    greet(blk, grp, cycle, cores, pos, line)
 
     def t_copy(i, d):
         dest = lax.rem(blk + d, cycle)
@@ -796,7 +1003,14 @@
     def s_here(r, s):
         return pltpu.make_async_copy(*s_ends(r, s), s_local.at[r])
 
+    mix_copies = [
+        send(mix_hbm, mix.at[blk], p_send.at[d - 1], p_recv.at[d - 1], lax.rem(blk + d, cycle), grp)
+        for d in range(1, cycle)
+    ]
     for i in range(chunks):
+        if i == min(kept, chunks - 1):
+            for copy in mix_copies:
+                copy.start()
         for d in range(cycle):
             t_copy(i, d).start()
         if i < per_half:
@@ -869,10 +1083,12 @@
         )
 
     def compute(kind, i):
-        if kind == "g":
+        if kind == "m" or i >= kept:
             await_inputs(i)
         if (kind, i) == ("g", 0):
             loads[0].wait()
+            for copy in mix_copies:
+                copy.wait()
         if (kind, i) == ("m", 0):
             loads[1].wait()
             loads[2].wait()
@@ -959,21 +1175,10 @@
         )
 
     low = pos < line // 2
-    items = [("g", i) for i in range(chunks)] + [("m", i) for i in range(kept)]
+    items = [("m", i) for i in range(kept)] + [("g", i) for i in range(chunks)]
     for k in range(len(items) + 3):
-        if k < len(items):
+        if k < len(items) and k != kept:
             compute(*items[k])
-        if k == len(items) and kept < chunks:
-            if not kept:
-                loads[1].wait()
-                loads[2].wait()
-
-            def body(group, carry):
-                for i in range(kept, chunks):
-                    terms[group, pl.ds((i - kept) * step, step), :] = out_term(i, group)
-                return carry
-
-            lax.fori_loop(0, line * cores, body, 0)
         if 0 <= k - 1 < len(items):
             fold(*items[k - 1])
             flow(*items[k - 1], low)
@@ -981,6 +1186,21 @@
             flow(*items[k - 2], jnp.logical_not(low))
         if 0 <= k - 3 < len(items):
             final(*items[k - 3])
+        if k == kept:
+            compute(*items[k])
+        if kept < chunks and k >= len(items) - 1:
+            if not kept and k == len(items) - 1:
+                loads[1].wait()
+                loads[2].wait()
+            part = line * cores // 4
+
+            def body(n, carry):
+                group = (k - len(items) + 1) * part + n
+                for i in range(kept, chunks):
+                    terms[group, pl.ds((i - kept) * step, step), :] = out_term(i, group)
+                return carry
+
+            lax.fori_loop(0, part, body, 0)
 
     for s in range(cycle):
         here = (s == blk) & (owner == grp)
@@ -1045,7 +1265,7 @@
             jax.ShapeDtypeStruct((groups, rest * step, wide), kind),
         ],
         scratch_shapes=[
-            pltpu.VMEM(mix.shape, kind),
+            pltpu.VMEM((cycle,) + mix.shape, kind),
             pltpu.VMEM(t_out.shape, kind),
             pltpu.VMEM(s_out.shape, kind),
             pltpu.VMEM((rows, t_width), kind),
@@ -1066,7 +1286,7 @@
         ]
         + line_sems(chunks)
         + line_sems(held)
-        + [dma((chunks, share)), dma((cycle, chunks // cores))],
+        + [dma((chunks, share)), dma((cycle, chunks // cores)), dma((cycle - 1,)), dma((cycle - 1,))],
         compiler_params=pltpu.CompilerParams(
             collective_id=2, has_side_effects=True, vmem_limit_bytes=VMEM_LIMIT
         ),
@@ -1080,65 +1300,29 @@
     t_query, t_key, t_value, t_out, s_query, s_key, s_value, s_out, segments, selection
 ):
     rows = t_query.shape[0]
-    cycle, cores = lax.axis_size("blk"), lax.axis_size("grp")
-    split = ("head", "grp")
-    groups = lax.axis_size("head") * cores
-    blk, grp = lax.axis_index("blk"), lax.axis_index("grp")
-    half = rows // cores
-    share = cycle // cores
-    per_blk = rows // BS
-    mine = per_blk // cores
+    cycle, cores, line = lax.axis_size("blk"), lax.axis_size("grp"), lax.axis_size("head")
     picks = selection.shape[1]
-
-    piece = s_out.shape[0] // cycle
-    s_rows = lax.dynamic_slice_in_dim(s_out, blk * piece, piece, 0)
-    s_rows = lax.all_gather(s_rows, split, axis=0, tiled=True)
 
     lanes = 128
     ints = jnp.concatenate(
         [segments.reshape(rows // lanes, lanes), jnp.pad(selection, ((0, 0), (0, lanes - picks)))]
     )
-    tq, tk, tv, pq, pk, pv, ints = arrive(
-        t_query, t_key, t_value, s_query, s_key, s_value, ints, cycle, cores
+    tq, tk, tv, pq, pk, pv, table, info, mix, blended = arrive(
+        t_query, t_key, t_value, t_out, s_query,
+        s_key.reshape(rows // BS, BS, -1), s_value.reshape(rows // BS, BS, -1),
+        s_out, ints, picks, (cycle, cores, line),
     )
-    s_rows, tq = lax.optimization_barrier((s_rows, tq))
-    seg_rows = rows // lanes
-    first_count = jnp.sum((ints[:, :seg_rows] == 0).astype(jnp.int32))
-    info = jnp.stack([first_count, grp, jnp.int32(cores)]).astype(jnp.int32)
-    chosen = lax.dynamic_slice_in_dim(ints[:, seg_rows:, :picks], grp * mine, mine, 1)
-    chosen = chosen.reshape(cycle * mine, picks)
-    at = chosen % per_blk
-    place = ((at // mine) * cycle + chosen // per_blk) * mine + at % mine
-    tables = (chosen, place, info)
-    pq = pq.reshape(cycle * half, HD)
-    pk, pv = pk.reshape(cycle * rows, HD), pv.reshape(cycle * rows, HD)
-
-    blended = pair_forward(per_blk, tables, pq, pk, pv)
-    tables, blended, tq = lax.optimization_barrier((tables, blended, tq))
-
-    mix = jnp.concatenate([dot(s_rows, t_out, NT), dot(s_rows, s_out, NT)], axis=1)
-    mix = lax.all_gather(mix.astype(jnp.bfloat16), "blk")
-
     whole = [x.reshape(cycle * rows, HD) for x in (tq, tk, tv)]
-    whole_heads = teacher(*whole, 1, (1, (0, 0, 0)), jnp.int32(0), first_count)
-
-    kept = 2
+    whole_heads = teacher(info, *whole, 1, (1, (0, 0, 0)))
+
+    kept = 3
     grads, near, terms = combine(
-        whole_heads.reshape(cycle, rows, HD), blended.reshape(cycle, half, HD), mix,
-        t_out, s_out, cycle, cores, groups // cores, kept,
+        whole_heads.reshape(cycle, rows, HD), blended, mix, t_out, s_out, cycle, cores, line, kept
     )
-    rest = lax.psum_scatter(terms, split, scatter_dimension=0, tiled=False)
-    grads = grads.reshape(cycle * half, HD)
-    dq, own, far = pair_backward(per_blk, cores, tables, pq, grads, pk, pv)
-    out = depart(
-        dq.reshape(cycle, half, HD),
-        own.reshape(2, cycle, half, HD),
-        far.reshape(2, cycle, half, HD),
-        cycle,
-        cores,
-    ).astype(jnp.float32)
-    mismatch = jnp.concatenate([near, rest.astype(jnp.float32)])
-    return (mismatch, out[0], out[1], out[2])
+    dq, own, far = pair_backward(table, info, picks, pq, grads, pk, pv)
+    *out, rest = depart(dq, own, far, terms, cycle, cores, line)
+    mismatch = jnp.concatenate([near, rest])
+    return (mismatch, *(x.astype(jnp.float32) for x in out))
 
 
 def on_device(t_query, t_key, t_value, t_out, s_query, s_key, s_value, s_out, segments, selection):
@@ -1176,19 +1360,19 @@
         ).reshape(row_count, 3 * heads * HD)
         packed = lax.all_to_all(packed, "blk", split_axis=1, concat_axis=0, tiled=True)
         packed, s_key, s_value = lax.optimization_barrier((packed, s_key, s_value))
+        start = jnp.stack([jnp.int32(0), first_count]).astype(jnp.int32)
         whole_heads = teacher(
-            packed, packed, packed, heads // cycle, (3, (0, 1, 2)), jnp.int32(0), first_count
+            start, packed, packed, packed, heads // cycle, (3, (0, 1, 2))
         )
         t_attn = lax.all_to_all(whole_heads, "blk", split_axis=0, concat_axis=1, tiled=True)
     else:
         t_attn = teacher(
+            info,
             t_query,
             lax.all_gather(t_key, "blk", axis=0, tiled=True),
             lax.all_gather(t_value, "blk", axis=0, tiled=True),
             heads,
             (1, (0, 0, 0)),
-            first_row,
-            first_count,
         )
 
     key_stack = jnp.concatenate([s_key] + [from_earlier(s_key, d) for d in range(1, cycle)])

time: 295 us -> 280 us (0.949)
  between operations: 13.9 us -> 0.69 us
  Pallas kernels: 259 us -> 271 us
  matrix products: 8.36 us -> 0 us
  local copies, waits for them, and re-layouts: 4.93 us -> 0.02 us
    pallas_call x1, Pallas kernels: 97.2 us -> 115 us  [combine(): pl.pallas_call(functools.partial(combine_kernel, cycle, cores, line, chun...]
    dot_general x2 -> x0, matrix products: 8.36 us -> none  [dot(): return lax.dot_general(a, b, dims, preferred_element_type=jnp.float32)]
    pallas_call x1, Pallas kernels: 33.7 us -> 26.1 us  [teacher(): pl.pallas_call(functools.partial(teacher_kernel, tile), grid_spec=pltpu.P...]
    pallas_call x4 -> x3, Pallas kernels: 128 us -> 130 us  [the longest x1 67.9 us: arrive(): pl.pallas_call(functools.partial(arrive_kernel, cycle, cores, line, picks...]
  transfers between devices with their start and end apart: 3 -> 0, of which waited for: 0 -> 0; matrix products, arithmetic and copies ran while one was open for 3% -> 0% of each run, Pallas kernels for 55% -> 0%
where the time goes in v4:
time: 280 us; the launch traced here: 279 us
  Pallas kernels  271 us (97%)
  other arithmetic  7.06 us (3%)
    pallas_call x1, Pallas kernels, combine(): pl.pallas_call(functools.partial(combine_kernel, cycle, cores, line, chun...  115 us
    pallas_call x1, Pallas kernels, arrive(): pl.pallas_call(functools.partial(arrive_kernel, cycle, cores, line, picks...  67.9 us
    pallas_call x1, Pallas kernels, depart(): pl.pallas_call(functools.partial(depart_kernel, cycle, cores, line, parts...  33.6 us
    pallas_call x1, Pallas kernels, pair_backward(): pl.pallas_call(functools.partial(pair_backward_kernel, picks, tokens // c...  28.1 us
    pallas_call x1, Pallas kernels, teacher(): pl.pallas_call(functools.partial(teacher_kernel, tile), grid_spec=pltpu.P...  26.1 us

profile of v4, /device:TPU:0, one launch (start us, length us, event | category | flops | bytes accessed | tf_op | source)
XLA Modules:
  0.0 278.5 jit_solution(14952048804489221310)
XLA Ops:
  0.6 1.3 pad_add_fusion.ints
  1.9 67.9 %shard_map.129 = (bf16[4,1024,128]{2,1,0:T(8,128)(2,1)}, bf16[4,1024,128]{2,1,0:T(8,128)(2,1)}, bf16[4,1024,128]{2,1,0:T(8,128)(2,1)}, bf16[4,512,128]{2,1,0:T(8...) custom-call(bf16[1024,512]{1,0:T(8,128)(2,1)} %tq.1, ...), custom_call_target="tpu_custom_call" | custom-call | tf_op jit(solution)/shard_map/pallas_call | solution.py:594
  69.9 26.1 %shard_map.130 = bf16[4096,128]{1,0:T(8,128)(2,1)} custom-call(s32[4]{0:T(128)} %get-tuple-element.24.info_ref, bf16[4096,128]{1,0:T(8,128)(2,1)} %bitcast.11, bf16[4096,128]{1,0:T(8,128)(2,1)} %bitcast.12, bf16[4096,128]{1,0:T(8,128)(2,1)} %bitcast.13), custom_call_target="tpu_custom_call" | custom-call | flops 4294967296 | bytes 4194304 | tf_op jit(solution)/shard_map/pallas_call | solution.py:82
  96.0 115.0 %shard_map.131 = (bf16[4,512,128]{2,1,0:T(8,128)(2,1)}, f32[768,512]{1,0:T(8,128)}, bf16[8,256,512]{2,1,0:T(8,128)(2,1)}) custom-call(bf16[4,1024,128]{2,1,0:T(8,128)(2,1)} %bitcast.7, bf16[4,512,128]{2,1,0:T(8,128)(2,1)} %get-tuple-element.28.heads_s, bf16[512,768]{1,0:T(8,128)(2,1)} %get-tuple-element.29.mix_hbm, bf16[512,4096]{1,0:T(8,128)(2,1)} %t_hbm.3, ...), custom_call_target="tpu_custom_call" | custom-call | bytes 268435456 | tf_op jit(solution)/shard_map/pallas_call | solution.py:1258
  211.1 28.1 %shard_map.132 = (bf16[4,512,128]{2,1,0:T(8,128)(2,1)}, f32[2,4,512,128]{3,2,1,0:T(8,128)}, bf16[2,4,512,128]{3,2,1,0:T(8,128)(2,1)}) custom-call(s32[4,24,128]{2,1,0:T(8,128)} %get-tuple-element.31.table, s32[4]{0:T(128)} %get-tuple-element.24.info_ref, bf16[4,512,128]{2,1,0:T(8,128)(2,1)} %get-tuple-element.32.q_ref, ...), custom_call_target="tpu_custom_call" | custom-call | flops 34359738368 | bytes 4194304 | tf_op jit(solution)/shard_map/pallas_call | solution.py:937
  239.2 0.0 copy-start
  239.2 33.6 %shard_map.133 = (bf16[1024,256]{1,0:T(8,128)(2,1)}, bf16[1024,256]{1,0:T(8,128)(2,1)}, bf16[1024,256]{1,0:T(8,128)(2,1)}, f32[256,512]{1,0:T(8,128)}) custom-call(bf16[4,512,128]{2,1,0:T(8,128)(2,1)} %get-tuple-element.36.dq, f32[2,4,512,128]{3,2,1,0:T(8,128)} %get-tuple-element.37.own, bf16[2,4,512,128]{3,2,1,0:T(8,128)(2,1)} %get-tuple-element.38.far, ...), custom_call_target="tpu_custom_call" | custom-call | tf_op jit(solution)/shard_map/pallas_call | solution.py:803
  272.7 0.0 copy-done
  272.7 0.0 copy-start.3
  272.7 0.0 copy-start.2
  272.8 2.6 pad_maximum_fusion
  275.4 0.0 copy-done.3
  275.4 0.0 copy-start.1
  275.4 1.0 convert_element_type.9
  276.4 0.0 copy-done.2
  276.4 1.0 convert_element_type.10
  277.5 0.0 copy-done.1
  277.5 1.0 convert_element_type.11
Async XLA Ops:
  239.2 33.6 %copy-start = (f32[768,512]{1,0:T(8,128)S(1)}, f32[768,512]{1,0:T(8,128)}, u32[]{:S(2)}) copy-start(f32[768,512]{1,0:T(8,128)} %get-tuple-element.30) | copy-start | bytes 4718596
  272.7 2.6 copy-start.3
  272.7 3.7 %copy-start.2 = (bf16[1024,256]{1,0:T(8,128)(2,1)S(1)}, bf16[1024,256]{1,0:T(8,128)(2,1)}, u32[]{:S(2)}) copy-start(bf16[1024,256]{1,0:T(8,128)(2,1)} %get-tuple-element.42) | copy-start | bytes 1572868
  275.4 2.1 copy-start.1
